TPU v7x, 32 devices: a whole 2x2x4 slice. The times are simulated.
32 devices in a mesh: member: 8 (over y, x, core), tile: 4 (over z).
Axes of the slice: x: 2, y: 2, z: 4, core: 2. Of those that a mesh axis runs over, the one named last changes fastest.
Arguments:
- node_fine: int32 [8, 12], P('member'), may hold values from 0 to 8
- node_coarse: int32 [32, 12], P('member'), may hold values from 0 to 8
- weight_fine: int32 [8], P('member'), may hold values from -3 to 3
- weight_coarse: int32 [32], P('member'), may hold values from -3 to 3
- mode_x: float32 [12, 64], replicated, may hold values from -1 to 1
- mode_y: float32 [12, 512], replicated, may hold values from -1 to 1
- mode_z: float32 [12, 32], replicated, may hold values from -1 to 1
- source_fine: float32 [64, 32, 512], P('tile'), may hold values from -12 to 12
- source_coarse: float32 [32, 16, 256], P(None, None, 'tile'), may hold values from -6 to 6
Outputs:
- combined: float32 [32, 16, 256], P('member', None, 'tile')
All inputs are finite; a program needn't handle non-finite values.
Results may differ from a plain program's by a relative error of at most 0.00026.
Values sent between devices are 32-bit elements; how exact they have to be, the bound alone decides.
No kernel may reach another device: no remote copies, remote signals or barrier semaphores. Data moves between devices by JAX's collectives and lax.ppermute only.
A program may use at most 192 MiB of HBM per device.

v0:
```python
import math

import jax
import jax.numpy as jnp
from jax import lax
from jax.sharding import PartitionSpec as P

NODES = 9
SWEEPS = 3


CENTRE = 1.125
HALF_WIDTH = 0.875
SPREAD_RATIO = CENTRE / HALF_WIDTH


def extended(block, sides, width):
    for axis, dim in sides:
        count = lax.axis_size(axis)
        forward = [(i, i + 1) for i in range(count - 1)]
        backward = [(target, source) for source, target in forward]
        low = lax.ppermute(
            lax.slice_in_dim(block, block.shape[dim] - width, None, axis=dim), axis, forward
        )
        high = lax.ppermute(lax.slice_in_dim(block, 0, width, axis=dim), axis, backward)
        block = jnp.concatenate([low, block, high], axis=dim)
    return block


def sweep_factors(sweep_count):
    previous = 1.0 / SPREAD_RATIO
    factors = []
    for _ in range(sweep_count - 1):
        current = 1.0 / (2.0 * SPREAD_RATIO - previous)
        factors.append((current * previous, 2.0 * current / HALF_WIDTH))
        previous = current
    return factors


def shifted(tensor, spatial, along_dim, offset):
    for current in spatial:
        begin_at = offset if current == along_dim else 1
        tensor = lax.slice_in_dim(
            tensor, begin_at, tensor.shape[current] - 2 + begin_at, axis=current
        )
    return tensor


def diagonal_of(cond_pad, spatial):
    centre = shifted(cond_pad, spatial, -1, 1)
    running = jnp.zeros_like(centre)
    for along_dim in spatial:
        for offset in (0, 2):
            running = running + 0.5 * (centre + shifted(cond_pad, spatial, along_dim, offset))
    return running


def apply_op(field_pad, cond_pad, spatial):
    centre_k = shifted(cond_pad, spatial, -1, 1)
    centre_v = shifted(field_pad, spatial, -1, 1)
    running = jnp.zeros_like(centre_v * centre_k)
    for along_dim in spatial:
        for offset in (0, 2):
            coupling = 0.5 * (centre_k + shifted(cond_pad, spatial, along_dim, offset))
            running = running + coupling * (
                centre_v - shifted(field_pad, spatial, along_dim, offset)
            )
    return running


def node_values(node_index):
    return jnp.cos(math.pi * node_index.astype(jnp.float32) / (NODES - 1))


def pair_mean(modes):
    return 0.5 * (modes[:, 0::2] + modes[:, 1::2])


def log_field(values, along_x, along_z, along_y):
    weighted = (along_x.T * values)[:, None, :] * along_z.T[None, :, :]
    flattened = weighted.reshape(weighted.shape[0] * weighted.shape[1], weighted.shape[2])
    product = jnp.dot(flattened, along_y, precision=lax.Precision.HIGHEST)
    return product.reshape(weighted.shape[0], weighted.shape[1], along_y.shape[1])


def log_batch(values, along_x, along_z, along_y):
    weighted = (along_x.T[None, :, :] * values[:, None, :])[:, :, None, :] * along_z.T[
        None, None, :, :
    ]
    shape_in = weighted.shape
    flattened = weighted.reshape(shape_in[0] * shape_in[1] * shape_in[2], shape_in[3])
    product = jnp.dot(flattened, along_y, precision=lax.Precision.HIGHEST)
    return product.reshape(shape_in[0], shape_in[1], shape_in[2], along_y.shape[1])


def restrict(tensor):
    blocks = tensor.reshape(
        tensor.shape[0] // 2, 2, tensor.shape[1] // 2, 2, tensor.shape[2] // 2, 2
    )
    return blocks.sum(axis=(1, 3, 5)) * 0.125


def trim_dim(tensor, trim_depth, along_dim):
    return lax.slice_in_dim(
        tensor, trim_depth, tensor.shape[along_dim] - trim_depth, axis=along_dim
    )


def pad_other(tensor, halo_dim, spatial):
    widths = []
    for position in range(tensor.ndim):
        if position in spatial and position != halo_dim:
            widths.append((1, 1))
        else:
            widths.append((0, 0))
    return jnp.pad(tensor, widths)


def smooth_deep(source_ext, cond_pad, halo_dim, spatial, inside, reach_cells, factors):
    diagonal = diagonal_of(cond_pad, spatial)
    safe_diag = diagonal + (1.0 - inside)
    update = source_ext / (CENTRE * safe_diag) * inside
    result = trim_dim(update, reach_cells, halo_dim)
    residual = source_ext
    extent = reach_cells
    for keep_part, push_part in factors:
        cond_part = trim_dim(cond_pad, reach_cells + 1 - extent, halo_dim)
        applied = apply_op(pad_other(update, halo_dim, spatial), cond_part, spatial)
        residual = trim_dim(residual, 1, halo_dim) - applied
        extent = extent - 1
        trim_depth = reach_cells - extent
        fresh = keep_part * trim_dim(update, 1, halo_dim) + push_part * residual / trim_dim(
            safe_diag, trim_depth, halo_dim
        )
        update = fresh * trim_dim(inside, trim_depth, halo_dim)
        result = result + trim_dim(update, extent, halo_dim)
    return result


def body(
    node_fine,
    node_coarse,
    weight_fine,
    weight_coarse,
    mode_x,
    mode_y,
    mode_z,
    source_fine,
    source_coarse,
):
    factors = sweep_factors(SWEEPS)
    reach_cells = SWEEPS - 1
    tile_place = lax.axis_index("tile")
    strip_width = source_fine.shape[0]
    coarse_width = source_coarse.shape[2]
    mode_xc = pair_mean(mode_x)
    mode_yc = pair_mean(mode_y)
    mode_zc = pair_mean(mode_z)
    extent = reach_cells + 1
    padded_x = jnp.pad(mode_x, ((0, 0), (extent, extent)))
    mode_slab = lax.dynamic_slice_in_dim(
        padded_x, tile_place * strip_width, strip_width + 2 * extent, 1
    )
    global_x = (
        tile_place * strip_width - extent + jnp.arange(strip_width + 2 * extent, dtype=jnp.int32)
    )
    inside_x = ((global_x >= 0) & (global_x < mode_x.shape[1])).astype(jnp.float32)
    conduct = (
        jnp.exp(log_field(node_values(node_fine[0]), mode_slab, mode_z, mode_y))
        * inside_x[:, None, None]
    )
    cond_fine = pad_other(conduct, 0, (0, 1, 2))
    padded_y = jnp.pad(mode_yc, ((0, 0), (extent, extent)))
    mode_strip = lax.dynamic_slice_in_dim(
        padded_y, tile_place * coarse_width, coarse_width + 2 * extent, 1
    )
    global_y = (
        tile_place * coarse_width - extent + jnp.arange(coarse_width + 2 * extent, dtype=jnp.int32)
    )
    inside_y = ((global_y >= 0) & (global_y < mode_yc.shape[1])).astype(jnp.float32)
    conduct_c = (
        jnp.exp(log_batch(node_values(node_coarse), mode_xc, mode_zc, mode_strip)) * inside_y
    )
    cond_coarse = pad_other(conduct_c, 3, (1, 2, 3))
    fine_ext = extended(source_fine, (("tile", 0),), reach_cells)
    fine_inside = trim_dim(inside_x, 1, 0)[:, None, None]
    fine_result = smooth_deep(fine_ext, cond_fine, 0, (0, 1, 2), fine_inside, reach_cells, factors)
    coarse_ext = extended(source_coarse, (("tile", 2),), reach_cells)
    coarse_inside = trim_dim(inside_y, 1, 0)[None, None, None, :]
    coarse_result = smooth_deep(
        coarse_ext[None], cond_coarse, 3, (1, 2, 3), coarse_inside, reach_cells, factors
    )
    fine_part = weight_fine[0].astype(jnp.float32) * restrict(fine_result)
    arrived = lax.all_to_all(fine_part, "tile", split_axis=2, concat_axis=0, tiled=True)
    coarse_part = jnp.tensordot(
        weight_coarse.astype(jnp.float32), coarse_result, axes=1, precision=lax.Precision.HIGHEST
    )
    summed = arrived + coarse_part
    return lax.psum_scatter(summed, "member", scatter_dimension=0, tiled=True)


def solution(mesh):
    return jax.shard_map(
        body,
        mesh=mesh,
        in_specs=(
            P("member", None),
            P("member", None),
            P("member"),
            P("member"),
            P(),
            P(),
            P(),
            P("tile", None, None),
            P(None, None, "tile"),
        ),
        out_specs=P("member", None, "tile"),
        check_vma=False,
    )
```

profile of v0, /device:TPU:0, one launch (start us, length us, event | category | flops | bytes accessed | tf_op | source)
XLA Modules:
  0.0 194.3 jit_solution(10056728130827275311)
XLA Ops:
  6.5 1.7 fusion.159
  8.3 5.6 %collective-permute-start = (f32[2,32,512]{2,1,0:T(8,128)}, f32[2,32,512]{2,1,0:T(8,128)}, u32[]{:S(2)}, u32[]{:S(2)}) collective-permute-start(f32[2,32,512]{2,1,0:T(8,128)} %get-tuple-element.14), channel_id=1, source_target_pairs={{0,1},{1,2},{2,3},{4,5},{5,6},{6,7},{8,9},{9,10},{10,11},{12,13},{... | collective-permute-start | bytes 393224 | tf_op jit(solution)/shard_map/ppermute | solution.py:22
  13.9 1.3 collective-permute-start.1
  15.2 1.2 fusion.160
  16.3 4.6 %collective-permute-start.2 = (f32[32,16,2]{2,1,0:T(8,128)S(1)}, f32[32,16,2]{2,1,0:T(8,128)S(1)}, u32[]{:S(2)}, u32[]{:S(2)}) collective-permute-start(f32[32,16,2]{2,1,0:T(8,128)S(1)} %get-tuple-element.15), channel_id=1, source_target_pairs={{0,1},{1,2},{2,3},{4,5},{5,6},{6,7},{8,9},{9,10},{10,11},{12,13},{... | collective-permute-start | bytes 12296 | tf_op jit(solution)/shard_map/ppermute | solution.py:22
  20.9 1.3 collective-permute-start.3
  22.2 0.1 slice.637
  22.4 0.1 slice.638
  22.5 0.5 slice.641
  23.0 0.5 slice.642
  23.5 0.1 slice.639
  23.6 0.1 slice.640
  23.8 0.1 multiply_bitcast_fusion.2
  23.9 0.1 copy.29
  24.0 0.1 broadcast_subtract_fusion.1
  24.1 0.1 copy.34
  24.3 0.1 slice_bitcast_fusion.2
  24.3 1.7 fusion
  26.1 0.1 broadcast_multiply_fusion.1
  26.2 1.9 fusion.1
  29.0 1.0 collective-permute-done.3
  30.0 0.2 pad_maximum_fusion
  30.2 0.1 copy.33
  30.3 0.2 fusion.161
  30.5 0.1 slice_bitcast_fusion
  30.7 0.1 copy.35
  30.8 1.7 divide_multiply_fusion.1
  32.5 4.2 %fusion.128 = (f32[4,32,16,66]{3,1,2,0:T(8,128)S(1)}, f32[4,32,16,66]{3,1,2,0:T(8,128)S(1)}) fusion(f32[4,32,16,68]{3,1,2,0:T(8,128)S(1)} %get-tuple-element.12, f32[4,32,16,68]{3,1,2,0:T(8,128)S(1)} %get-tuple-element.11, f32[66]{0:T(128)S(1)} %slice_bitcast_fusion.2, f32[4,32,16,70]{3,1,2,0:T(8,128)S(1)} %fusion.1, f32[32,16,66]{2,0,1:T(8,128)S(1)} %copy.35), kind=kLoop, calls=%fused_computation.183 | loop fusion | flops 4730880 | bytes 10781184 | tf_op jit(solution)/shard_map/mul | solution.py:135
  36.7 4.5 %fusion.133 = f32[4,32,16,64]{3,1,2,0:T(8,128)S(1)} fusion(f32[4,32,16,68]{3,1,2,0:T(8,128)S(1)} %get-tuple-element.11, f32[4,32,16,68]{3,1,2,0:T(8,128)S(1)} %get-tuple-element.12, f32[4,32,16,66]{3,1,2,0:T(8,128)S(1)} %get-tuple-element.9, f32[4,32,16,70]{3,1,2,0:T(8,128)S(1)} %fusion.1, f32[4,32,16,66]{3,1,2,0:T(8,128)S(1)} %get-tuple-element.10, ...), kind=kLoop, calls=%fused_computation.193 | loop fusion | flops 4849664 | bytes 12059136 | tf_op jit(solution)/shard_map/add | solution.py:136
  41.2 0.9 constant_dynamic-update-slice_fusion.2
  42.2 0.1 constant_dynamic-update-slice_fusion.1
  42.3 0.9 constant_dynamic-update-slice_fusion
  43.2 1.2 divide_multiply_fusion
  44.4 2.9 %fusion.35 = (f32[18,32,512]{2,1,0:T(8,128)S(1)}, f32[18,32,512]{2,1,0:T(8,128)S(1)}) fusion(f32[20,32,512]{2,1,0:T(8,128)S(1)} %get-tuple-element.8, f32[20,32,512]{2,1,0:T(8,128)S(1)} %get-tuple-element.7, f32[18]{0:T(128)S(1)} %slice.617, f32[22,32,512]{2,1,0:T(8,128)S(1)} %fusion, f32[20,32,512]{2,1,0:T(8,128)S(1)} %constant_dynamic-update-slice_fusion), kind=kLoop, calls=%fused_computation.81 | loop fusion | flops 10321920 | bytes 14549504 | tf_op jit(solution)/shard_map/mul | solution.py:135
  47.3 2.7 %fusion.139 = f32[16,32,512]{2,1,0:T(8,128)S(1)} fusion(f32[20,32,512]{2,1,0:T(8,128)S(1)} %get-tuple-element.7, f32[20,32,512]{2,1,0:T(8,128)S(1)} %get-tuple-element.8, f32[18,32,512]{2,1,0:T(8,128)S(1)} %get-tuple-element.5, f32[22,32,512]{2,1,0:T(8,128)S(1)} %fusion, f32[18,32,512]{2,1,0:T(8,128)S(1)} %get-tuple-element.6, f32[16]{0:T(128)S(1)} %slice.634), kind=kLoop, calls=%fused_computation.206 | loop fusion | flops 9699328 | bytes 13107712 | tf_op jit(solution)/shard_map/add | solution.py:136
  50.0 68.4 %reshape.50 = f32[8,2,16,2,256,2]{5,4,3,2,1,0:T(8,128)} reshape(f32[16,32,512]{2,1,0:T(8,128)S(1)} %fusion.139) | data formatting | bytes 2097152 | tf_op jit(solution)/shard_map/reshape | solution.py:97
  118.4 20.8 %reduce_sum.9 = f32[8,16,256]{2,1,0:T(8,128)S(1)} reduce(f32[8,2,16,2,256,2]{5,4,3,2,1,0:T(8,128)} %reshape.50, f32[]{:T(128)} %constant.18.clone.1), dimensions={1,3,5}, to_apply=%region_0.1 | reduce | flops 229376 | bytes 1179652 | tf_op jit(solution)/shard_map/reduce_sum | solution.py:100
  139.2 0.4 copy.30
  139.6 1.0 reshape.55
  140.7 4.9 %all-to-all-start = ((f32[4,1,8192]{2,1,0:T(1,128)}), f32[4,1,8192]{2,1,0:T(1,128)S(1)}, u32[]{:S(2)}, u32[]{:S(2)}) async-start(f32[4,1,8192]{2,1,0:T(1,128)} %reshape.55), calls=%async_computation | async-start | bytes 262144 | tf_op jit(solution)/shard_map/all_to_all | solution.py:194
  145.6 2.6 %fusion.140 = f32[1,32,16,64]{3,0,2,1:T(1,128)S(1)} fusion(f32[4,32,16,64]{3,1,2,0:T(8,128)S(1)} %fusion.133, s32[4]{0:T(128)S(1)} %copy-done.6), kind=kOutput, calls=%fused_computation.207 | convolution fusion | flops 1572868 | bytes 655376 | tf_op jit(solution)/shard_map/dot_general | solution.py:195
  148.1 3.3 %all-to-all-done = f32[4,1,8192]{2,1,0:T(1,128)S(1)} async-done(((f32[4,1,8192]{2,1,0:T(1,128)}), f32[4,1,8192]{2,1,0:T(1,128)S(1)}, u32[]{:S(2)}, u32[]{:S(2)}) %all-to-all-start) | async-done | bytes 131104 | tf_op jit(solution)/shard_map/all_to_all | solution.py:194
  151.5 0.5 broadcast.125
  152.0 1.0 reduce
  153.0 0.4 reshape.56
  153.4 0.4 copy.40
  153.8 0.7 bitcast_add_fusion
  154.6 32.9 %reduce-scatter.2.cloned.1.call-done = f32[4,16,64]{2,1,0:T(8,128)} async-done(((f32[32,16,64]{2,1,0:T(8,128)}), f32[4,16,64]{2,1,0:T(8,128)}) %reduce-scatter.2.cloned.1.call-update) | async-done | bytes 16400 | tf_op jit(solution)/shard_map/reduce_scatter | solution.py:199
  (34 shorter events, 0.5 us)
Async XLA Ops:
  6.5 15.7 %copy-start.4 = (f32[12,64]{1,0:T(8,128)S(1)}, f32[12,64]{1,0:T(8,128)}, u32[]{:S(2)}) copy-start(f32[12,64]{1,0:T(8,128)} %param.13) | copy-start | bytes 9220
  6.5 16.0 %copy-start.2 = (f32[12,512]{1,0:T(8,128)S(1)}, f32[12,512]{1,0:T(8,128)}, u32[]{:S(2)}) copy-start(f32[12,512]{1,0:T(8,128)} %param.14) | copy-start | bytes 73732
  6.5 17.0 %copy-start.3 = (f32[12,32]{1,0:T(8,128)S(1)}, f32[12,32]{1,0:T(8,128)}, u32[]{:S(2)}) copy-start(f32[12,32]{1,0:T(8,128)} %param.15) | copy-start | bytes 4612
  6.5 17.2 %copy-start.7 = (s32[1,12]{1,0:T(1,128)S(1)}, s32[1,12]{1,0:T(1,128)}, u32[]{:S(2)}) copy-start(s32[1,12]{1,0:T(1,128)} %param.9) | copy-start | bytes 148
  6.5 17.5 %copy-start.5 = (s32[4,12]{1,0:T(4,128)S(1)}, s32[4,12]{1,0:T(4,128)}, u32[]{:S(2)}) copy-start(s32[4,12]{1,0:T(4,128)} %param.10) | copy-start | bytes 580
  8.3 32.9 %collective-permute-start = (f32[2,32,512]{2,1,0:T(8,128)}, f32[2,32,512]{2,1,0:T(8,128)}, u32[]{:S(2)}, u32[]{:S(2)}) collective-permute-start(f32[2,32,512]{2,1,0:T(8,128)} %get-tuple-element.14), channel_id=1, source_target_pairs={{0,1},{1,2},{2,3},{4,5},{5,6},{6,7},{8,9},{9,10},{10,11},{12,13},{... | collective-permute-start | bytes 393224 | tf_op jit(solution)/shard_map/ppermute | solution.py:22
  13.9 28.4 %collective-permute-start.1 = (f32[2,32,512]{2,1,0:T(8,128)}, f32[2,32,512]{2,1,0:T(8,128)}, u32[]{:S(2)}, u32[]{:S(2)}) collective-permute-start(f32[2,32,512]{2,1,0:T(8,128)} %get-tuple-element.13), channel_id=1, source_target_pairs={{1,0},{2,1},{3,2},{5,4},{6,5},{7,6},{9,8},{10,9},{11,10},{13,12},{... | collective-permute-start | bytes 393224 | tf_op jit(solution)/shard_map/ppermute | solution.py:25
  16.3 12.6 %collective-permute-start.2 = (f32[32,16,2]{2,1,0:T(8,128)S(1)}, f32[32,16,2]{2,1,0:T(8,128)S(1)}, u32[]{:S(2)}, u32[]{:S(2)}) collective-permute-start(f32[32,16,2]{2,1,0:T(8,128)S(1)} %get-tuple-element.15), channel_id=1, source_target_pairs={{0,1},{1,2},{2,3},{4,5},{5,6},{6,7},{8,9},{9,10},{10,11},{12,13},{... | collective-permute-start | bytes 12296 | tf_op jit(solution)/shard_map/ppermute | solution.py:22
  20.9 9.1 %collective-permute-start.3 = (f32[32,16,2]{2,1,0:T(8,128)S(1)}, f32[32,16,2]{2,1,0:T(8,128)S(1)}, u32[]{:S(2)}, u32[]{:S(2)}) collective-permute-start(f32[32,16,2]{2,1,0:T(8,128)S(1)} %get-tuple-element.16), channel_id=1, source_target_pairs={{1,0},{2,1},{3,2},{5,4},{6,5},{7,6},{9,8},{10,9},{11,10},{13,12},{... | collective-permute-start | bytes 12296 | tf_op jit(solution)/shard_map/ppermute | solution.py:25
  24.3 5.7 %copy-start = (f32[32,16,64]{2,1,0:T(8,128)S(1)}, f32[32,16,64]{2,1,0:T(8,128)}, u32[]{:S(2)}) copy-start(f32[32,16,64]{2,1,0:T(8,128)} %param.17) | copy-start | bytes 393220
  36.7 5.5 %copy-start.1 = (f32[16,32,512]{2,1,0:T(8,128)S(1)}, f32[16,32,512]{2,1,0:T(8,128)}, u32[]{:S(2)}) copy-start(f32[16,32,512]{2,1,0:T(8,128)} %param.16) | copy-start | bytes 3145732
  139.2 6.4 %copy-start.6 = (s32[4]{0:T(128)S(1)}, s32[4]{0:T(128)}, u32[]{:S(2)}) copy-start(s32[4]{0:T(128)} %param.12) | copy-start | bytes 52
  140.7 10.8 %all-to-all-start = ((f32[4,1,8192]{2,1,0:T(1,128)}), f32[4,1,8192]{2,1,0:T(1,128)S(1)}, u32[]{:S(2)}, u32[]{:S(2)}) async-start(f32[4,1,8192]{2,1,0:T(1,128)} %reshape.55), calls=%async_computation | async-start | bytes 262144 | tf_op jit(solution)/shard_map/all_to_all | solution.py:194
  145.6 41.9 %reduce-scatter.2.cloned.1.call-start = ((), (), s32[]{:S(2)}) async-start(), calls=%async_computation.2 | async-start | bytes 294912 | tf_op jit(solution)/shard_map/reduce_scatter | solution.py:199
Sparse Core Ops, SparseCore 0:
  154.7 32.7 reduce-scatter.1
where the time goes:
time: 195 us; the launch traced here: 194 us
  local copies, waits for them, and re-layouts  78.2 us (40%)
  other arithmetic  40.5 us (21%)
  waiting for transfers between devices  37.3 us (19%)
  starting transfers between devices  17.7 us (9%)
  between operations  14.4 us (7%)
  matrix products  6.21 us (3%)
    reshape x1, local copies, waits for them, and re-layouts, restrict(): tensor.reshape(tensor.shape[0] // 2, 2, tensor.shape[1] // 2, 2, tensor.s...  68.4 us
    reduce_scatter x1, waiting for transfers between devices, body(): return lax.psum_scatter(summed, 'member', scatter_dimension=0, tiled=True)  32.9 us
    reduce_sum x1, other arithmetic, restrict(): return blocks.sum(axis=(1, 3, 5)) * 0.125  20.8 us
    ppermute x2, starting transfers between devices, extended(): lax.ppermute(lax.slice_in_dim(block, block.shape[dim] - width, None, axis...  10.2 us
    add x2, other arithmetic, smooth_deep(): result = result + trim_dim(update, extent, halo_dim)  7.19 us
    mul x2, other arithmetic, smooth_deep(): update = fresh * trim_dim(inside, trim_depth, halo_dim)  7.12 us
    all_to_all x1, starting transfers between devices, body(): lax.all_to_all(fine_part, 'tile', split_axis=2, concat_axis=0, tiled=True)  4.92 us
  transfers between devices with their start and end apart: 6, of which 3 were waited for; matrix products, arithmetic and copies ran while one was open for 11% of the time, Pallas kernels for 0%

commit v1 on v0

v1 whole, which is shorter than its diff:
```python
import math

import jax
import jax.numpy as jnp
import numpy as np
from jax import lax
from jax.experimental import pallas as pl
from jax.experimental.pallas import tpu as pltpu
from jax.sharding import PartitionSpec as P

NODES = 9
SWEEPS = 3
CENTRE = 1.125
HALF_WIDTH = 0.875
SPREAD_RATIO = CENTRE / HALF_WIDTH

LANES = 128
HALO = SWEEPS
EDGE = 4
PAD = 8
FAR = -2048.0


def sweep_factors(sweep_count):
    previous = 1.0 / SPREAD_RATIO
    factors = []
    for _ in range(sweep_count - 1):
        current = 1.0 / (2.0 * SPREAD_RATIO - previous)
        factors.append((current * previous, 2.0 * current / HALF_WIDTH))
        previous = current
    return factors


(A1, B1), (A2, B2) = sweep_factors(SWEEPS)
FIRST = (A1 + (CENTRE - 1.0) * B1) / B1
KEEP0 = (1.0 - B2 * A1 / B1) / (B1 * B2)
KEEP1 = (1.0 + A2 + B2 / B1 - B2) / B2
SCALE = 2.0 / CENTRE * B1 * B2


def pieces(value):
    high = value.astype(jnp.bfloat16)
    rest = value - high.astype(jnp.float32)
    mid = rest.astype(jnp.bfloat16)
    low = (rest - mid.astype(jnp.float32)).astype(jnp.bfloat16)
    return high, mid, low


def outer_pieces(value):
    high = lax.reduce_precision(value, 8, 7)
    rest = value - high
    mid = lax.reduce_precision(rest, 8, 7)
    low = lax.reduce_precision(rest - mid, 8, 7)
    return tuple(part.astype(jnp.bfloat16) for part in (high, mid, low))


def smooth_kernel(
    groups, nx, ny, nz, pair,
    par_ref, sel_ref, zt_ref, xb_ref, yt_ref, src_ref, spread_ref, ym_ref, rt_ref, xin_ref,
    out_ref,
    yz_ref, c_ref, kz_ref, q_ref, d_ref, e_ref, u_ref,
):
    height = ny + 2 * EDGE
    lane = lax.broadcasted_iota(jnp.int32, (height, LANES), 1) % nz
    is_last = lane == nz - 1
    is_first = lane == 0
    mid = pl.ds(PAD, height)
    up = pl.ds(PAD + 1, height)
    down = pl.ds(PAD - 1, height)

    named = lax.dot_general(
        par_ref[...], sel_ref[...], (((0,), (0,)), ((), ())),
        precision=lax.Precision.HIGHEST, preferred_element_type=jnp.float32,
    )
    weights = []
    for g in range(groups):
        block = named[:, g * LANES:(g + 1) * LANES]
        yz_ref[g] = block * zt_ref[...]
        weights.append(block[14:15, :])

    def conduct(i, carry):
        row = xb_ref[i]
        for g in range(groups):
            high, middle, low = pieces(row * yz_ref[g])
            stacked = jnp.concatenate([high, middle, low, high, middle, high], axis=0)
            power = jnp.dot(yt_ref[...], stacked, preferred_element_type=jnp.float32)
            c_ref[g, i, mid, :] = jnp.exp(power)
        return carry

    lax.fori_loop(0, nx + 2 * HALO, conduct, 0)

    def start(i, carry):
        source = jnp.concatenate(pieces(src_ref[i - 1]), axis=0)
        force = lax.dot_general(
            source, spread_ref[...], (((0,), (0,)), ((), ())),
            preferred_element_type=jnp.float32,
        )
        mask = ym_ref[...] * xin_ref[i]
        for g in range(groups):
            c0 = c_ref[g, i, mid, :]
            zp = jnp.where(is_last, 0.0, pltpu.roll(c0, LANES - 1, 1))
            zm = jnp.where(is_first, 0.0, pltpu.roll(c0, 1, 1))
            total = (
                6.0 * c0 + (c_ref[g, i - 1, mid, :] + c_ref[g, i + 1, mid, :])
                + (c_ref[g, i, up, :] + c_ref[g, i, down, :]) + (zp + zm)
            )
            q = mask / (total + 1e-30)
            q_ref[g, i, mid, :] = q
            d_ref[g, i, mid, :] = force * q
            kz_ref[g, i, mid, :] = jnp.where(is_last, 0.0, c0 + zp)
        return carry

    lax.fori_loop(1, nx + 2 * HALO - 1, start, 0)

    def around(g, i, v_ref, mid, up, down):
        c0 = c_ref[g, i, mid, :]
        v0 = v_ref[g, i, mid, :]
        kz = kz_ref[g, i, mid, :]
        near = (c0 + c_ref[g, i + 1, mid, :]) * v_ref[g, i + 1, mid, :]
        near += (c0 + c_ref[g, i - 1, mid, :]) * v_ref[g, i - 1, mid, :]
        near += (c0 + c_ref[g, i, up, :]) * v_ref[g, i, up, :]
        near += (c0 + c_ref[g, i, down, :]) * v_ref[g, i, down, :]
        near += kz * pltpu.roll(v0, LANES - 1, 1)
        near += pltpu.roll(kz * v0, 1, 1)
        return v0, q_ref[g, i, mid, :] * near

    def first(i, carry):
        for g in range(groups):
            v0, near = around(g, i, d_ref, mid, up, down)
            e_ref[g, i, mid, :] = FIRST * v0 + near
        return carry

    lax.fori_loop(2, nx + 2 * HALO - 2, first, 0)

    inner = pl.ds(PAD + EDGE, ny)
    inner_up = pl.ds(PAD + EDGE + 1, ny)
    inner_down = pl.ds(PAD + EDGE - 1, ny)
    step = 2 if pair else 1
    scale = SCALE * (0.125 if pair else 1.0)

    def second(k, carry):
        total = None
        for s in range(step):
            i = HALO + step * k + s
            for g in range(groups):
                v0, near = around(g, i, e_ref, inner, inner_up, inner_down)
                u = KEEP0 * d_ref[g, i, inner, :] + KEEP1 * v0 + near
                u = u * (scale * weights[g])
                total = u if total is None else total + u
        u_ref[...] = total
        if pair:
            total = u_ref[pl.ds(0, ny // 2, stride=2), :] + u_ref[pl.ds(1, ny // 2, stride=2), :]
        stacked = jnp.concatenate(pieces(total), axis=1)
        out_ref[k] = lax.dot_general(
            rt_ref[...], stacked, (((1,), (1,)), ((), ())),
            preferred_element_type=jnp.float32,
        )
        return carry

    lax.fori_loop(0, nx // step, second, 0)


def smooth(par, sel, zt, xb, yt, src, ym, xin, nx, ny, nz, pair):
    groups = sel.shape[1] // LANES
    height = ny + 2 * EDGE
    members = LANES // nz
    spread = np.tile(np.eye(nz, dtype=np.float32), (3, members))
    out_z = nz // 2 if pair else nz
    rt = np.tile(np.eye(out_z, dtype=np.float32).repeat(nz // out_z, axis=1), (1, 3 * members))
    vmem = pl.BlockSpec(memory_space=pltpu.VMEM)
    smem = pl.BlockSpec(memory_space=pltpu.SMEM)
    nxe = nx + 2 * HALO
    grid = pltpu.VMEM((groups, nxe, height + 2 * PAD, LANES), jnp.float32)

    def kernel(*refs):
        smooth_kernel(groups, nx, ny, nz, pair, *refs)

    step = 2 if pair else 1
    return pl.pallas_call(
        kernel,
        out_shape=jax.ShapeDtypeStruct((nx // step, out_z, ny // step), jnp.float32),
        in_specs=[vmem] * 9 + [smem],
        out_specs=vmem,
        scratch_shapes=[pltpu.VMEM((groups, 16, LANES), jnp.float32), grid, grid, grid, grid, grid,
                        pltpu.VMEM((ny, LANES), jnp.float32)],
        compiler_params=pltpu.CompilerParams(vmem_limit_bytes=60 << 20),
        name="fine_smooth" if pair else "coarse_smooth",
    )(par, sel, zt, xb, yt, src, jnp.asarray(spread, jnp.bfloat16), ym,
      jnp.asarray(rt, jnp.bfloat16), xin)


def selector(devices, block, first_row, per_device, nz):
    members = devices * per_device
    out = np.zeros((devices * block, members * nz), np.float32)
    for k in range(members):
        row = (k // per_device) * block + first_row + k % per_device
        out[row, k * nz:(k + 1) * nz] = 1.0
    return out


def tables(mode_x, mode_y, mode_z, x0, nx, y0, ny, nz):
    terms = mode_x.shape[0]
    nxe, height = nx + 2 * HALO, ny + 2 * EDGE
    px = jnp.pad(mode_x, ((0, 0), (HALO, HALO)))
    px = lax.dynamic_slice_in_dim(px, x0, nxe, 1)
    gx = x0 - HALO + jnp.arange(nxe, dtype=jnp.int32)
    x_in = ((gx >= 0) & (gx < mode_x.shape[1])).astype(jnp.float32)
    xcol = jnp.concatenate(
        [px.T, jnp.ones((nxe, 1), jnp.float32), ((1.0 - x_in) * FAR)[:, None],
         jnp.zeros((nxe, 2), jnp.float32)], axis=1)
    xb = jnp.broadcast_to(xcol[:, :, None], (nxe, terms + 4, LANES))
    py = jnp.pad(mode_y, ((0, 0), (EDGE, EDGE)))
    py = lax.dynamic_slice_in_dim(py, y0, height, 1)
    gy = y0 - EDGE + jnp.arange(height, dtype=jnp.int32)
    y_in = ((gy >= 0) & (gy < mode_y.shape[1])).astype(jnp.float32)
    ycol = jnp.concatenate(
        [py.T, ((1.0 - y_in) * FAR)[:, None], jnp.ones((height, 1), jnp.float32),
         jnp.zeros((height, 2), jnp.float32)], axis=1)
    high, middle, low = outer_pieces(ycol)
    yt = jnp.concatenate([high, high, high, middle, middle, low], axis=1)
    ym = jnp.broadcast_to(y_in[:, None], (height, LANES))
    zt = jnp.concatenate(
        [jnp.tile(mode_z, (1, LANES // nz)), jnp.ones((2, LANES), jnp.float32),
         jnp.zeros((2, LANES), jnp.float32)], axis=0)
    return zt, xb, yt, ym, x_in


def pair_mean(modes):
    return 0.5 * (modes[:, 0::2] + modes[:, 1::2])


def solution(mesh):
    members, tiles = mesh.shape["member"], mesh.shape["tile"]
    per_strip = members // tiles
    assert per_strip == 2 and members == tiles * per_strip and tiles >= 4
    axes = ("member", "tile")

    def flat(b, a, t):
        return (b * per_strip + a) * tiles + t

    def quarter(b, t):
        return b ^ t ^ jnp.where(t < tiles // 2, tiles - 1, 0)

    def quarter_py(b, t):
        return b ^ t ^ (tiles - 1 if t < tiles // 2 else 0)

    def chain(bit, sign):
        pairs = []
        for b in range(tiles):
            for t in range(tiles):
                for a, move in ((0, sign), (1, -sign)):
                    to = t + move
                    if 0 <= to < tiles:
                        pairs.append((flat(b, a, t), flat(b ^ bit, a, to)))
                    else:
                        pairs.append((flat(b, a, t), flat(b ^ bit, 1 - a, t)))
        return pairs

    def receiver(b, a, t, bit, sign):
        to = t + jnp.where(a == 0, sign, -sign)
        ok = (to >= 0) & (to < tiles)
        return b ^ bit, jnp.where(ok, a, 1 - a), jnp.where(ok, to, t)

    def body(node_fine, node_coarse, weight_fine, weight_coarse, mode_x, mode_y, mode_z,
             source_fine, source_coarse):
        m, t = lax.axis_index("member"), lax.axis_index("tile")
        a, b = m % per_strip, m // per_strip
        terms = mode_x.shape[0]
        strip, nz, _ = source_fine.shape
        nx = mode_x.shape[1] // members
        ny = mode_y.shape[1] // tiles
        cx, cz, cy = source_coarse.shape[0] // members, source_coarse.shape[1], source_coarse.shape[2]
        reach = SWEEPS - 1
        height = ny + 2 * EDGE
        n_fine, n_coarse = node_fine.shape[0], node_coarse.shape[0]
        block = -(-(n_fine + n_coarse) // 8) * 8

        nodes = jnp.concatenate([node_fine, node_coarse], axis=0)
        values = jnp.cos(math.pi * nodes.astype(jnp.float32) / (NODES - 1))
        weight = jnp.concatenate([weight_fine, weight_coarse]).astype(jnp.float32)[:, None]
        par = jnp.concatenate(
            [values, jnp.ones((n_fine + n_coarse, 2), jnp.float32), weight,
             jnp.zeros((n_fine + n_coarse, 1), jnp.float32)], axis=1)
        width = terms + 4
        par = jnp.pad(par, ((0, block - par.shape[0]), (0, LANES - width)))

        near = lax.ppermute(par, "member", [(i, i ^ 1) for i in range(members)])
        par = jnp.concatenate([par, near], axis=0)

        fine_wide = jnp.pad(source_fine, ((0, 0), (0, 0), (EDGE, EDGE)))
        coarse_wide = jnp.pad(source_coarse, ((reach, reach), (0, 0), (0, 0)))

        def coarse_rows(bit, sign):
            rb, ra, _ = receiver(b, a, t, bit, sign)
            low_side = jnp.where(a == 0, sign, -sign) < 0
            rows = lax.dynamic_slice(
                coarse_wide, (cx * (rb * per_strip + ra), 0, jnp.where(low_side, 0, cy - reach)),
                (cx + 2 * reach, cz, reach))
            return rows.transpose(2, 0, 1).reshape(reach, -1)

        bits = []
        bit = tiles // 2
        while bit:
            bits.append(bit)
            bit //= 2
        rb, ra, rt = receiver(b, a, t, bits[0], 1)
        planes = lax.dynamic_slice(
            fine_wide, (jnp.where(a == 0, strip - reach, 0), 0, ny * quarter(rb, rt)),
            (reach, nz, height)).reshape(reach * nz, height)
        edge = coarse_rows(bits[0], 1)
        count, rows = par.shape[0], edge.shape[0]
        wide = max(height, LANES, edge.shape[1])
        sent = jnp.concatenate(
            [jnp.pad(part, ((0, 0), (0, wide - part.shape[1]))) for part in (planes, par, edge)],
            axis=0)
        got = lax.ppermute(sent, axes, chain(bits[0], 1))
        planes = got[:reach * nz, :height].reshape(reach, nz, height)
        par = jnp.concatenate([par, got[reach * nz:reach * nz + count, :LANES]], axis=0)
        edge_one = got[reach * nz + count:, :edge.shape[1]]
        edge = coarse_rows(bits[1], -1)
        count = par.shape[0]
        got = lax.ppermute(jnp.concatenate([par, edge], axis=0), axes, chain(bits[1], -1))
        par = jnp.concatenate([par, got[:count]], axis=0)
        edge_two = got[count:]
        for bit in bits[2:]:
            got = lax.ppermute(par, "member", [(i, i ^ (bit * per_strip)) for i in range(members)])
            par = jnp.concatenate([par, got], axis=0)
        par = par[:, :width]

        q = quarter(b, t)
        own = lax.dynamic_slice(
            fine_wide, (jnp.where(a == 0, 0, strip - nx - reach), 0, ny * q), (nx + reach, nz, height))
        src = jnp.where(a == 0, jnp.concatenate([planes, own], axis=0),
                        jnp.concatenate([own, planes], axis=0))
        zt, xb, yt, ym, x_in = tables(
            mode_x, mode_y, mode_z, t * strip + a * nx, nx, q * ny, ny, nz)
        sel = jnp.asarray(selector(members, block, 0, n_fine, nz))
        fine = smooth(par, sel, zt, xb, yt, src, ym, x_in, nx, ny, nz, True)
        pairs = [(flat(b_, a_, t_), flat(t_, a_, quarter_py(b_, t_)))
                 for b_ in range(tiles) for a_ in range(per_strip) for t_ in range(tiles)]
        arrived = lax.ppermute(fine, axes, pairs)

        own = lax.dynamic_slice_in_dim(coarse_wide, cx * m, cx + 2 * reach, 0)

        def unpack(edge):
            return edge.reshape(reach, cx + 2 * reach, cz).transpose(1, 2, 0)

        low = unpack(jnp.where(a == 0, edge_one, edge_two))
        high = unpack(jnp.where(a == 0, edge_two, edge_one))
        gap = jnp.zeros(own.shape[:2] + (EDGE - reach,), jnp.float32)
        src = jnp.concatenate([gap, low, own, high, gap], axis=2)
        zt, xb, yt, ym, x_in = tables(
            pair_mean(mode_x), pair_mean(mode_y), pair_mean(mode_z), cx * m, cx, t * cy, cy, cz)
        sel = jnp.asarray(selector(members, block, n_fine, n_coarse, cz))
        coarse = smooth(par, sel, zt, xb, yt, src, ym, x_in, cx, cy, cz, False)
        return arrived + coarse

    return jax.shard_map(
        body,
        mesh=mesh,
        in_specs=(
            P("member", None), P("member", None), P("member"), P("member"),
            P(), P(), P(), P("tile", None, None), P(None, None, "tile"),
        ),
        out_specs=P("member", None, "tile"),
        check_vma=False,
    )
```

time: 195 us -> 52 us (0.27)
  local copies, waits for them, and re-layouts: 78.2 us -> 15 us
  other arithmetic: 40.5 us -> 6.57 us
  waiting for transfers between devices: 37.3 us -> 3.48 us
  Pallas kernels: 0 us -> 17.8 us
  between operations: 14.4 us -> 1 us
  starting transfers between devices: 17.7 us -> 7.46 us
  matrix products: 6.21 us -> 0 us
    reshape x1 -> x2, local copies, waits for them, and re-layouts: 68.4 us -> 0.12 us  [coarse_rows(): return rows.transpose(2, 0, 1).reshape(reach, -1)]
    reduce_scatter x1 -> x0, waiting for transfers between devices: 32.9 us -> none  [body(): return lax.psum_scatter(summed, 'member', scatter_dimension=0, tiled=True)]
    reduce_sum x1 -> x0, other arithmetic: 20.8 us -> none  [restrict(): return blocks.sum(axis=(1, 3, 5)) * 0.125]
    pallas_call x0 -> x2, Pallas kernels: none -> 17.8 us  [smooth(): pl.pallas_call(kernel, out_shape=jax.ShapeDtypeStruct((nx // step, out_z,...]
    mul x8 -> x4, other arithmetic: 10.2 us -> 0.04 us  [the longest x2 0.02 us: tables(): (1.0 - y_in) * FAR]
    add x3 -> x1, other arithmetic: 7.92 us -> 1.38 us  [body(): return arrived + coarse]
    dot_general x3 -> x0, matrix products: 6.21 us -> none  [the longest x1 2.55 us: body(): jnp.tensordot(weight_coarse.astype(jnp.float32), coarse_result, axes=1, p...]
    ppermute x4, starting transfers between devices: 12.7 us -> 7.46 us  [the longest x1 3.68 us: body(): got = lax.ppermute(sent, axes, chain(bits[0], 1))]
  transfers between devices with their start and end apart: 6 -> 4, of which waited for: 3 -> 1; matrix products, arithmetic and copies ran while one was open for 11% -> 30% of each run, Pallas kernels for 0% -> 14%
where the time goes in v1:
time: 52 us; the launch traced here: 51.3 us
  Pallas kernels  17.8 us (34%)
  local copies, waits for them, and re-layouts  15 us (29%)
  starting transfers between devices  7.46 us (14%)
  other arithmetic  6.57 us (13%)
  waiting for transfers between devices  3.48 us (7%)
  between operations  1 us (2%)
    pallas_call x2, Pallas kernels, smooth(): pl.pallas_call(kernel, out_shape=jax.ShapeDtypeStruct((nx // step, out_z,...  17.8 us
    slice x6, local copies, waits for them, and re-layouts, pair_mean(): return 0.5 * (modes[:, 0::2] + modes[:, 1::2])  5.7 us
    ppermute x1, starting transfers between devices, body(): got = lax.ppermute(sent, axes, chain(bits[0], 1))  3.68 us
    ppermute x1, waiting for transfers between devices, body(): lax.ppermute(jnp.concatenate([par, edge], axis=0), axes, chain(bits[1], -1))  3.48 us
    ppermute x1, starting transfers between devices, body(): arrived = lax.ppermute(fine, axes, pairs)  2.22 us
    concatenate x2, local copies, waits for them, and re-layouts, tables(): yt = jnp.concatenate([high, high, high, middle, middle, low], axis=1)  1.48 us
    broadcast_in_dim x2, local copies, waits for them, and re-layouts, tables(): xb = jnp.broadcast_to(xcol[:, :, None], (nxe, terms + 4, LANES))  1.44 us
    broadcast_in_dim x2, local copies, waits for them, and re-layouts, tables(): ym = jnp.broadcast_to(y_in[:, None], (height, LANES))  1.39 us
  transfers between devices with their start and end apart: 4, of which 1 were waited for; matrix products, arithmetic and copies ran while one was open for 30% of the time, Pallas kernels for 14%

profile of v1, /device:TPU:0, one launch (start us, length us, event | category | flops | bytes accessed | tf_op | source)
XLA Modules:
  0.0 51.3 jit_solution(15492054544382619667)
XLA Ops:
  0.7 0.7 %pad_add_fusion = s32[5,1]{0,1:T(1,128)S(1)} fusion(s32[4,1]{0,1:T(1,128)} %bitcast.32, s32[1,1]{0,1:T(1,128)} %bitcast.25), kind=kLoop, calls=%fused_computation.59 | loop fusion | flops 5 | bytes 40 | tf_op jit(solution)/shard_map/concatenate | solution.py:280
  1.5 0.1 copy.37
  1.7 0.7 %fusion.7 = f32[5,12]{1,0:T(8,128)S(1)} fusion(s32[4,12]{1,0:T(4,128)} %param.16, s32[1,12]{1,0:T(1,128)} %param.15), kind=kLoop, calls=%fused_computation.39 | loop fusion | flops 180 | bytes 480 | tf_op jit(solution)/shard_map/cos | solution.py:279
  2.6 0.5 collective-permute-start
  3.1 1.2 %slice.44 = f32[12,256]{1,0:T(8,128)S(1)} slice(f32[12,512]{1,0:T(8,128)} %param.20), slice={[0:12:1], [0:512:2]} | slice | bytes 24576 | tf_op jit(solution)/shard_map/slice | solution.py:229
  4.3 1.2 %slice.45 = f32[12,256]{1,0:T(8,128)S(1)} slice(f32[12,512]{1,0:T(8,128)} %param.20), slice={[0:12:1], [1:512:2]} | slice | bytes 24576 | tf_op jit(solution)/shard_map/slice | solution.py:229
  5.5 0.8 %slice.42 = f32[12,32]{1,0:T(8,128)S(1)} slice(f32[12,64]{1,0:T(8,128)} %param.19), slice={[0:12:1], [0:64:2]} | slice | bytes 3072 | tf_op jit(solution)/shard_map/slice | solution.py:229
  6.3 0.8 %slice.43 = f32[12,32]{1,0:T(8,128)S(1)} slice(f32[12,64]{1,0:T(8,128)} %param.19), slice={[0:12:1], [1:64:2]} | slice | bytes 3072 | tf_op jit(solution)/shard_map/slice | solution.py:229
  7.2 0.8 %slice.40 = f32[12,16]{1,0:T(8,128)S(1)} slice(f32[12,32]{1,0:T(8,128)} %param.21), slice={[0:12:1], [0:32:2]} | slice | bytes 1536 | tf_op jit(solution)/shard_map/slice | solution.py:229
  8.0 0.8 %slice.41 = f32[12,16]{1,0:T(8,128)S(1)} slice(f32[12,32]{1,0:T(8,128)} %param.21), slice={[0:12:1], [1:32:2]} | slice | bytes 1536 | tf_op jit(solution)/shard_map/slice | solution.py:229
  9.0 0.1 fusion.5
  9.1 0.1 copy.45
  9.2 0.1 copy.46
  9.4 0.1 tile.21
  9.4 0.7 %tile.8 = f32[12,4,32]{2,1,0:T(4,128)S(1)} broadcast(f32[12,32]{1,0:T(8,128)} %param.21), dimensions={0,2} | broadcast | bytes 7680 | tf_op jit(solution)/shard_map/tile | solution.py:223
  10.1 0.1 tile.9
  10.2 0.8 %fusion.4 = f32[136,12]{0,1:T(8,128)S(1)} fusion(s32[]{:T(128)S(6)} %select_n.114, f32[12,512]{1,0:T(8,128)} %param.20), kind=kLoop, calls=%fused_computation.22 | loop fusion | bytes 31108 | tf_op jit(solution)/shard_map/transpose | solution.py:217
  11.1 0.1 copy.41
  11.2 0.1 copy.42
  11.3 0.1 dynamic-slice_bitcast_fusion.1
  11.4 0.2 pad_dynamic-slice_fusion
  11.6 0.1 pad_dynamic-slice_fusion.1
  11.7 0.7 %copy-done.1 = f32[32,16,64]{2,1,0:T(8,128)S(1)} copy-done((f32[32,16,64]{2,1,0:T(8,128)S(1)}, f32[32,16,64]{2,1,0:T(8,128)}, u32[]{:S(2)}) %copy-start.1) | copy-done | bytes 131096
  12.4 0.1 dynamic-slice_bitcast_fusion
  12.5 0.7 %maximum_maximum_fusion.3 = (f32[16,128]{1,0:T(8,128)}, f32[16,128]{1,0:T(8,128)}) fusion(f32[12,128]{1,0:T(8,128)S(1)} %tile.21, f32[16]{0:T(128)S(1)} %pad.70.clone, f32[16]{0:T(128)S(1)} %pad.85.clone, f32[12,128]{1,0:T(8,128)S(1)} %tile.9), kind=kLoop, calls=%fused_computation.30 | loop fusion | flops 8192 | bytes 28800 | tf_op jit(solution)/shard_map/concatenate | solution.py:222
  13.4 0.1 pad_dynamic-slice_fusion.4
  13.5 0.5 %and_convert_fusion.1.refs_9_ = f32[10]{0:T(128)} fusion(s32[]{:T(128)S(6)} %sub.87), kind=kLoop, calls=%fused_computation.42 | loop fusion | flops 50 | bytes 44 | tf_op jit(solution)/shard_map/convert_element_type | solution.py:207
  14.1 3.7 %collective-permute-start.1 = (f32[82,136]{1,0:T(8,128)S(1)}, f32[82,136]{1,0:T(8,128)S(1)}, u32[]{:S(2)}, u32[]{:S(2)}) collective-permute-start(f32[82,136]{1,0:T(8,128)S(1)} %select_maximum_fusion), channel_id=1, source_target_pairs={{0,17},{4,16},{1,18},{5,20},{2,19},{6,21},{3,23},{7,22},{8,25},{12... | collective-permute-start | bytes 133832 | tf_op jit(solution)/shard_map/ppermute | solution.py:316
  17.8 0.6 %and_convert_fusion.5.refs_9_ = f32[14]{0:T(128)} fusion(s32[]{:T(128)S(6)} %sub.80), kind=kLoop, calls=%fused_computation.46 | loop fusion | flops 70 | bytes 60 | tf_op jit(solution)/shard_map/convert_element_type | solution.py:207
  18.5 0.1 copy.44
  18.5 0.1 copy.40
  18.6 0.7 %concatenate.87.refs_4_ = bf16[72,96]{1,0:T(8,128)(2,1)} concatenate(bf16[72,16]{1,0:T(8,128)(2,1)S(1)} %get-tuple-element.18, bf16[72,16]{1,0:T(8,128)(2,1)S(1)} %get-tuple-element.18, bf16[72,16]{1,0:T(8,128)(2,1)S(1)} %get-tuple-element.18, bf16[72,16]{1,0:T(8,128)(2,1)S(1)} %get-tuple-element.16, bf16[72,16]{1,0:T(8,128)(2,1)S(1)} %get-tuple-element.16, ...), dimensions={1} | concatenate | bytes 27648 | tf_op jit(solution)/shard_map/concatenate | solution.py:220
  19.4 0.7 %concatenate.81.refs_4_ = bf16[136,96]{1,0:T(8,128)(2,1)} concatenate(bf16[136,16]{1,0:T(8,128)(2,1)S(1)} %get-tuple-element.17, bf16[136,16]{1,0:T(8,128)(2,1)S(1)} %get-tuple-element.17, bf16[136,16]{1,0:T(8,128)(2,1)S(1)} %get-tuple-element.17, bf16[136,16]{1,0:T(8,128)(2,1)S(1)} %get-tuple-element.12, bf16[136,16]{1,0:T(8,128)(2,1)S(1)} %get-tuple-element.12, ...), dimensions={1} | concatenate | bytes 52224 | tf_op jit(solution)/shard_map/concatenate | solution.py:220
  20.1 1.1 %collective-permute-start.2 = (f32[34,128]{1,0:T(8,128)S(1)}, f32[34,128]{1,0:T(8,128)S(1)}, u32[]{:S(2)}, u32[]{:S(2)}) collective-permute-start(f32[34,128]{1,0:T(8,128)S(1)} %pad_maximum_fusion.3), channel_id=1, source_target_pairs={{0,12},{4,13},{1,8},{5,14},{2,9},{6,15},{3,10},{7,11},{8,4},{12,5}... | collective-permute-start | bytes 52232 | tf_op jit(solution)/shard_map/ppermute | solution.py:322
  21.2 0.8 %maximum_select_fusion.refs_5_ = f32[12,32,136]{2,1,0:T(8,128)} fusion(f32[10,32,136]{2,1,0:T(8,128)S(1)} %pad_dynamic-slice_fusion, f32[2,32,136]{2,1,0:T(8,128)S(1)} %bitcast.31, pred[]{:T(512)S(6)} %eq.4), kind=kLoop, calls=%fused_computation.2 | loop fusion | flops 156672 | bytes 417793 | tf_op jit(solution)/shard_map/jit(_where)/select_n | solution.py:333
  22.0 3.5 %collective-permute-done.2 = f32[34,128]{1,0:T(8,128)S(1)} collective-permute-done((f32[34,128]{1,0:T(8,128)S(1)}, f32[34,128]{1,0:T(8,128)S(1)}, u32[]{:S(2)}, u32[]{:S(2)}) %collective-permute-start.2) | collective-permute-done | bytes 17440 | tf_op jit(solution)/shard_map/ppermute | solution.py:322
  25.4 0.6 %pad_maximum_fusion.refs_0_ = f32[64,16]{1,0:T(8,128)} fusion(f32[32,128]{1,0:T(8,128)S(1)} %slice.49, f32[16,128]{1,0:T(8,128)S(1)} %slice.48, f32[8,128]{1,0:T(8,128)S(1)} %collective-permute-done, f32[8,128]{1,0:T(8,128)S(1)} %pad.36), kind=kLoop, calls=%fused_computation.17 | loop fusion | flops 3072 | bytes 36864 | tf_op jit(solution)/shard_map/concatenate | solution.py:323
  26.1 0.7 %broadcast_in_dim.14.refs_3_ = f32[14,16,128]{2,1,0:T(8,128)} broadcast(f32[14,16]{1,0:T(8,128)S(1)} %copy.40), dimensions={0,1} | broadcast | bytes 115584 | tf_op jit(solution)/shard_map/broadcast_in_dim | solution.py:211
  26.8 0.7 %broadcast_in_dim.16.refs_7_ = f32[136,128]{1,0:T(8,128)} broadcast(f32[136]{0:T(256)S(1)} %and_convert_fusion.6), dimensions={0} | broadcast | bytes 70176 | tf_op jit(solution)/shard_map/broadcast_in_dim | solution.py:221
  27.5 10.4 %fine_smooth.1 = f32[4,16,64]{2,1,0:T(8,128)} custom-call(f32[64,16]{1,0:T(8,128)} %pad_maximum_fusion.refs_0_, f32[64,256]{1,0:T(8,128)} %constant.131.clone.refs_1_, f32[16,128]{1,0:T(8,128)} %get-tuple-element.20.refs_2_, f32[14,16,128]{2,1,0:T(8,128)} %broadcast_in_dim.14.refs_3_, bf16[136,96]{1,0:T(8,128)(2,1)} %concatenate.81.refs_4_, ...), custom_call_target="tpu_custom_call" | custom-call | tf_op jit(solution)/shard_map/fine_smooth/pallas_call | solution.py:179
  37.9 2.2 %collective-permute-start.3 = (f32[4,16,64]{2,1,0:T(8,128)}, f32[4,16,64]{2,1,0:T(8,128)S(1)}, u32[]{:S(2)}, u32[]{:S(2)}) collective-permute-start(f32[4,16,64]{2,1,0:T(8,128)} %fine_smooth.1), channel_id=1, source_target_pairs={{0,3},{1,10},{2,18},{3,27},{4,7},{5,14},{6,22},{7,31},{8,2},{9,11}... | collective-permute-start | bytes 49160 | tf_op jit(solution)/shard_map/ppermute | solution.py:341
  40.2 0.1 copy.48
  40.3 0.1 copy.49
  40.4 0.8 %concatenate.88.refs_5_ = f32[8,16,72]{2,1,0:T(8,128)} concatenate(f32[8,16,2]{2,1,0:T(8,128)S(1)} %broadcast_in_dim.19, f32[8,16,2]{2,1,0:T(8,128)S(1)} %bitcast.29, f32[8,16,64]{2,1,0:T(8,128)S(1)} %pad_dynamic-slice_fusion.2, f32[8,16,2]{2,1,0:T(8,128)S(1)} %bitcast.30, f32[8,16,2]{2,1,0:T(8,128)S(1)} %broadcast_in_dim.19), dimensions={2} | concatenate | bytes 73728 | tf_op jit(solution)/shard_map/concatenate | solution.py:351
  41.2 0.7 %broadcast_in_dim.17.refs_3_ = f32[10,16,128]{2,1,0:T(8,128)} broadcast(f32[10,16]{1,0:T(8,128)S(1)} %copy.44), dimensions={0,1} | broadcast | bytes 82560 | tf_op jit(solution)/shard_map/broadcast_in_dim | solution.py:211
  41.9 0.7 %broadcast_in_dim.20.refs_7_ = f32[72,128]{1,0:T(8,128)} broadcast(f32[72]{0:T(128)S(1)} %and_convert_fusion.2), dimensions={0} | broadcast | bytes 37152 | tf_op jit(solution)/shard_map/broadcast_in_dim | solution.py:221
  42.6 7.4 %coarse_smooth.1 = f32[4,16,64]{2,1,0:T(8,128)} custom-call(f32[64,16]{1,0:T(8,128)} %pad_maximum_fusion.refs_0_, f32[64,512]{1,0:T(8,128)} %constant.134.clone.refs_1_, f32[16,128]{1,0:T(8,128)} %get-tuple-element.19.refs_2_, f32[10,16,128]{2,1,0:T(8,128)} %broadcast_in_dim.17.refs_3_, bf16[72,96]{1,0:T(8,128)(2,1)} %concatenate.87.refs_4_, ...), custom_call_target="tpu_custom_call" | custom-call | tf_op jit(solution)/shard_map/coarse_smooth/pallas_call | solution.py:179
  50.0 1.4 %add.191 = f32[4,16,64]{2,1,0:T(8,128)} add(f32[4,16,64]{2,1,0:T(8,128)S(1)} %collective-permute-done.3, f32[4,16,64]{2,1,0:T(8,128)} %coarse_smooth.1) | non-fusion elementwise | flops 4096 | bytes 49152 | tf_op jit(solution)/shard_map/add | solution.py:356
  (47 shorter events, 0.9 us)
Async XLA Ops:
  0.0 11.3 %copy-start.2 = (f32[12,64]{1,0:T(8,128)S(1)}, f32[12,64]{1,0:T(8,128)}, u32[]{:S(2)}) copy-start(f32[12,64]{1,0:T(8,128)} %param.19) | copy-start | bytes 9220
  0.0 11.4 %copy-start = (f32[16,32,512]{2,1,0:T(8,128)S(1)}, f32[16,32,512]{2,1,0:T(8,128)}, u32[]{:S(2)}) copy-start(f32[16,32,512]{2,1,0:T(8,128)} %param.22) | copy-start | bytes 3145732
  2.6 11.6 %collective-permute-start = (f32[8,128]{1,0:T(8,128)S(1)}, f32[8,128]{1,0:T(8,128)S(1)}, u32[]{:S(2)}, u32[]{:S(2)}) collective-permute-start(f32[8,128]{1,0:T(8,128)S(1)} %pad.36), channel_id=1, source_target_pairs={{0,4},{4,0},{8,12},{12,8},{16,20},{20,16},{24,28},{28,24},{1,5},{5... | collective-permute-start | bytes 12296 | tf_op jit(solution)/shard_map/ppermute | solution.py:287
  11.4 1.0 %copy-start.1 = (f32[32,16,64]{2,1,0:T(8,128)S(1)}, f32[32,16,64]{2,1,0:T(8,128)}, u32[]{:S(2)}) copy-start(f32[32,16,64]{2,1,0:T(8,128)} %param.23) | copy-start | bytes 393220
  14.1 6.0 %collective-permute-start.1 = (f32[82,136]{1,0:T(8,128)S(1)}, f32[82,136]{1,0:T(8,128)S(1)}, u32[]{:S(2)}, u32[]{:S(2)}) collective-permute-start(f32[82,136]{1,0:T(8,128)S(1)} %select_maximum_fusion), channel_id=1, source_target_pairs={{0,17},{4,16},{1,18},{5,20},{2,19},{6,21},{3,23},{7,22},{8,25},{12... | collective-permute-start | bytes 133832 | tf_op jit(solution)/shard_map/ppermute | solution.py:316
  20.1 5.3 %collective-permute-start.2 = (f32[34,128]{1,0:T(8,128)S(1)}, f32[34,128]{1,0:T(8,128)S(1)}, u32[]{:S(2)}, u32[]{:S(2)}) collective-permute-start(f32[34,128]{1,0:T(8,128)S(1)} %pad_maximum_fusion.3), channel_id=1, source_target_pairs={{0,12},{4,13},{1,8},{5,14},{2,9},{6,15},{3,10},{7,11},{8,4},{12,5}... | collective-permute-start | bytes 52232 | tf_op jit(solution)/shard_map/ppermute | solution.py:322
  37.9 12.0 %collective-permute-start.3 = (f32[4,16,64]{2,1,0:T(8,128)}, f32[4,16,64]{2,1,0:T(8,128)S(1)}, u32[]{:S(2)}, u32[]{:S(2)}) collective-permute-start(f32[4,16,64]{2,1,0:T(8,128)} %fine_smooth.1), channel_id=1, source_target_pairs={{0,3},{1,10},{2,18},{3,27},{4,7},{5,14},{6,22},{7,31},{8,2},{9,11}... | collective-permute-start | bytes 49160 | tf_op jit(solution)/shard_map/ppermute | solution.py:341

commit v2 on v0

v2 whole, which is shorter than its diff:
```python
import functools
import math

import jax
import jax.numpy as jnp
from jax import lax
from jax.experimental import pallas as pl
from jax.experimental.pallas import tpu as pltpu
from jax.sharding import PartitionSpec as P

NODES = 9
SWEEPS = 3
CENTRE = 1.125
HALF_WIDTH = 0.875
SPREAD_RATIO = CENTRE / HALF_WIDTH

LANES = 128
HALO = SWEEPS
REACH = SWEEPS - 1
EDGE = 4
PAD = 8
FAR = -2048.0
TERMS = 16
BLOCK = 8
UNROLL = (2, 2, 2, 2)


def sweep_factors(sweep_count):
    previous = 1.0 / SPREAD_RATIO
    factors = []
    for _ in range(sweep_count - 1):
        current = 1.0 / (2.0 * SPREAD_RATIO - previous)
        factors.append((current * previous, 2.0 * current / HALF_WIDTH))
        previous = current
    return factors


(A1, B1), (A2, B2) = sweep_factors(SWEEPS)
FIRST = A1 / B1 + CENTRE - 1.0
KEEP0 = (1.0 - B2 * A1 / B1) / (B1 * B2)
KEEP1 = (1.0 + A2 + B2 / B1 - B2) / B2
SHIFT = 0.5 * (FIRST + KEEP1)
REST = KEEP0 + KEEP1 * FIRST - SHIFT * SHIFT
SCALE = 2.0 / CENTRE * B1 * B2 * SHIFT ** 3
EXACT = lax.Precision.HIGHEST
ROWS = (((0,), (0,)), ((), ()))
COLUMNS = (((1,), (1,)), ((), ()))


def iota(shape, dim):
    return lax.broadcasted_iota(jnp.int32, shape, dim)


def pieces(value):
    high = value.astype(jnp.bfloat16)
    rest = value - high.astype(jnp.float32)
    mid = rest.astype(jnp.bfloat16)
    low = (rest - mid.astype(jnp.float32)).astype(jnp.bfloat16)
    return high, mid, low


def aligned(at):
    return at if isinstance(at, int) else pl.multiple_of(at, 8)


def quarter(b, t, tiles):
    return b ^ t ^ jnp.where(t < tiles // 2, tiles - 1, 0)


class Place:
    def __init__(self, tiles):
        m, t = lax.axis_index("member"), lax.axis_index("tile")
        self.tiles, self.m, self.t = tiles, m, t
        self.a, self.b = m % 2, m // 2
        self.half = self.a ^ (t % 2)

    def beside(self, outward):
        step = jnp.where(self.half == 1, 1, -1)
        to = self.t + (step if outward else -step)
        return jnp.where((to >= 0) & (to < self.tiles), to, self.t)


def prep_kernel(tiles, nx, ny, cx, bits, nf_ref, nc_ref, wf_ref, wc_ref, sf_ref, sc_ref,
                a_ref, b_ref, par_ref, plane_ref, sem):
    here = Place(tiles)
    strip, nz, full_y = sf_ref.shape
    full_x, cz, cy = sc_ref.shape
    height = ny + 2 * EDGE
    start = jnp.where(here.half == 1, strip - REACH, 0)
    copy = pltpu.make_async_copy(sf_ref.at[pl.ds(start, REACH)], plane_ref, sem)
    copy.start()

    def node_values(ref):
        nodes = ref[...]
        out = jnp.zeros(nodes.shape, jnp.float32)
        for k in range(NODES):
            out = jnp.where(nodes == k, math.cos(math.pi * k / (NODES - 1)), out)
        return out

    n_fine, terms = nf_ref.shape
    n_coarse = nc_ref.shape[0]
    row, lane = iota((BLOCK, LANES), 0), iota((BLOCK, LANES), 1)
    base = jnp.where((lane == terms) | (lane == terms + 1), 1.0, 0.0)
    for k in range(n_fine + n_coarse):
        weight = wf_ref[k] if k < n_fine else wc_ref[k - n_fine]
        base = jnp.where((row == k) & (lane == terms + 2), weight.astype(jnp.float32), base)
    par_ref[...] = base
    par_ref[0:n_fine, 0:terms] = node_values(nf_ref)
    par_ref[n_fine:n_fine + n_coarse, 0:terms] = node_values(nc_ref)

    rows = REACH * nz
    per_group = rows // cz
    spot = iota((rows, LANES), 1)

    def coarse_side(to_b, last, at):
        first = cx * (to_b * 2 + here.a) - REACH
        total = jnp.zeros((rows, LANES), jnp.float32)
        for group in range((cx + 2 * REACH) // per_group):
            parts = [sc_ref[jnp.clip(first + group * per_group + k, 0, full_x - 1)]
                     for k in range(per_group)]
            block = jnp.concatenate(parts, axis=0)
            block = jnp.concatenate([block] * (LANES // cy), axis=1)
            to = at + REACH * group
            shift = jnp.where(last, (to - cy + REACH) % LANES, to % LANES)
            block = pltpu.roll(block, shift, 1)
            total = jnp.where((spot >= to) & (spot < to + REACH), block, total)
        return total

    b_ref[0:rows, :] = coarse_side(here.b ^ bits[1], here.half == 0, EDGE * 2)
    edge = coarse_side(here.b ^ bits[0], here.half == 1, height % LANES)
    b_ref[rows:rows + BLOCK, :] = par_ref[...]
    a_ref[rows:rows + BLOCK, 0:LANES] = par_ref[...]

    target = quarter(here.b ^ bits[0], here.beside(True), tiles)
    shift = (EDGE + full_y - ny * target) % full_y
    copy.wait()
    for k in range(REACH):
        turned = pltpu.roll(plane_ref[k], shift, 1)
        part = slice(k * nz, (k + 1) * nz)
        for col in range(a_ref.shape[1] // LANES):
            block = turned[:, col * LANES:(col + 1) * LANES]
            if col == height // LANES:
                block = jnp.where(iota((nz, LANES), 1) < height % LANES, block, edge[part])
            a_ref[part, col * LANES:(col + 1) * LANES] = block


def factors(ratio, terms, nx, ny, nz, x0, y0, full_x, full_y, tx_ref, ty_ref,
            xb_ref, yt_ref, zt_ref):
    nxe, height = nx + 2 * HALO, ny + 2 * EDGE
    row = iota((TERMS, LANES), 0)
    xw = pltpu.roll(tx_ref[0], (ratio * (HALO - x0) + 2 * LANES) % LANES, 1)
    if ratio == 2:
        xw = 0.5 * (xw + pltpu.roll(xw, LANES - 1, 1))
    for i in range(nxe):
        at = x0 - HALO + i
        far = jnp.where((at < 0) | (at >= full_x), FAR, 0.0)
        col = jnp.broadcast_to(xw[:, ratio * i:ratio * i + 1], (TERMS, LANES))
        xb_ref[i] = jnp.where(row == terms, 1.0, jnp.where(row == terms + 1, far, col))
    span = -(-ratio * height // LANES) * LANES
    yw = pltpu.roll(ty_ref[...], (ratio * (EDGE - y0) + ratio * full_y) % (ratio * full_y), 1)
    yw = jnp.concatenate([yw[:, :span]] * 6, axis=0)
    pick = jnp.where(iota((height, span), 1) // ratio == iota((height, span), 0), 1.0 / ratio, 0.0)
    yt = lax.dot_general(pick, yw, COLUMNS, precision=EXACT, preferred_element_type=jnp.float32)
    lane = iota(yt.shape, 1)
    at = y0 - EDGE + iota(yt.shape, 0)
    far = jnp.where((at < 0) | (at >= full_y), FAR, 0.0)
    yt = jnp.where(lane % TERMS == terms, far, jnp.where(lane % TERMS == terms + 1, 1.0, yt))
    high, mid, low = (part.astype(jnp.float32) for part in pieces(yt))
    yt_ref[...] = jnp.where(lane < 3 * TERMS, high, jnp.where(lane < 5 * TERMS, mid, low)).astype(
        jnp.bfloat16)
    down, across = iota((LANES, LANES), 0), iota((LANES, LANES), 1)
    pick = jnp.where(down // ratio == across % nz, 1.0 / ratio, 0.0)
    zt = jnp.dot(tx_ref[1], pick, precision=EXACT, preferred_element_type=jnp.float32)
    zt_ref[...] = jnp.where((row == terms) | (row == terms + 1), 1.0, zt)


def members_of(pars, groups, nz, first_row, per_device, zt_ref, yz_ref):
    weights = []
    for par_ref in pars:
        size = par_ref.shape[0]
        for g in range(groups):
            member = (LANES // nz) * g + iota((size, LANES), 1) // nz
            source = BLOCK * (member // per_device) + first_row + member % per_device
            pick = jnp.where(iota((size, LANES), 0) == source, 1.0, 0.0)
            named = lax.dot_general(par_ref[:, 0:TERMS], pick, ROWS, precision=EXACT,
                                    preferred_element_type=jnp.float32)
            yz_ref[len(weights)] = named * zt_ref[...]
            weights.append(named[TERMS - 2:TERMS - 1, :])
    return weights


def chunks(count, size, run):
    def step(j, carry):
        for s in range(size):
            run(size * j + s)
        return carry

    whole = count // size
    lax.fori_loop(0, whole, step, 0)
    for k in range(whole * size, count):
        run(k)


def sweeps(groups, nx, ny, nz, x0, y0, full_x, full_y, pair, weights,
           xb_ref, yt_ref, yz_ref, force, c_ref, kz_ref, q_ref, d_ref, e_ref, u_ref, finish):
    nxe, height = nx + 2 * HALO, ny + 2 * EDGE

    def conduct(i, carry):
        row = xb_ref[i]
        for g in range(groups):
            high, middle, low = pieces(row * yz_ref[g])
            stacked = jnp.concatenate([high, middle, low, high, middle, high], axis=0)
            power = jnp.dot(yt_ref[...], stacked, preferred_element_type=jnp.float32)
            c_ref[g, i, pl.ds(PAD, height), :] = jnp.exp(power)
        return carry

    lax.fori_loop(0, nxe, conduct, 0, unroll=UNROLL[0])

    lane = iota((8, LANES), 1) % nz
    is_last, is_first = lane == nz - 1, lane == 0

    def start(k):
        at = aligned(PAD + 8 * k)
        here, up, down = pl.ds(at, 8), pl.ds(at + 1, 8), pl.ds(at - 1, 8)
        own = pl.ds(aligned(8 * k), 8)
        for g in range(groups):
            before, c0 = c_ref[g, 0, here, :], c_ref[g, 1, here, :]
            for i in range(1, nxe - 1):
                after = c_ref[g, i + 1, here, :]
                zp = jnp.where(is_last, 0.0, pltpu.roll(c0, LANES - 1, 1))
                zm = jnp.where(is_first, 0.0, pltpu.roll(c0, 1, 1))
                total = (6.0 * c0 + (before + after)) + (
                    (c_ref[g, i, up, :] + c_ref[g, i, down, :]) + (zp + zm))
                q = (1.0 / SHIFT) / total
                q_ref[g, i, here, :] = q
                d_ref[g, i, here, :] = force(i - 1, own) * q
                kz_ref[g, i, here, :] = jnp.where(is_last, 0.0, c0 + zp)
                before, c0 = c0, after

    chunks(height // 8, UNROLL[1], start)

    def clear_planes(planes):
        for g in range(groups):
            for i in planes:
                zero = jnp.zeros((height, LANES), jnp.float32)
                q_ref[g, i, pl.ds(PAD, height), :] = zero
                d_ref[g, i, pl.ds(PAD, height), :] = zero

    def clear_rows(at):
        for g in range(groups):
            for i in range(1, nxe - 1):
                zero = jnp.zeros((EDGE, LANES), jnp.float32)
                q_ref[g, i, pl.ds(PAD + at, EDGE), :] = zero
                d_ref[g, i, pl.ds(PAD + at, EDGE), :] = zero

    pl.when(x0 == 0)(lambda: clear_planes(range(1, HALO)))
    pl.when(x0 + nx == full_x)(lambda: clear_planes(range(nx + HALO, nxe - 1)))
    pl.when(y0 == 0)(lambda: clear_rows(0))
    pl.when(y0 + ny == full_y)(lambda: clear_rows(EDGE + ny))

    def walk(g, v_ref, first, last, here, up, down):
        c0, v0 = c_ref[g, first, here, :], v_ref[g, first, here, :]
        v_before = v_ref[g, first - 1, here, :]
        k_before = c_ref[g, first - 1, here, :] + c0
        for i in range(first, last):
            c_after, v_after = c_ref[g, i + 1, here, :], v_ref[g, i + 1, here, :]
            k_after = c0 + c_after
            kz = kz_ref[g, i, here, :]
            along_x = k_after * v_after + k_before * v_before
            along_y = ((c0 + c_ref[g, i, up, :]) * v_ref[g, i, up, :]
                       + (c0 + c_ref[g, i, down, :]) * v_ref[g, i, down, :])
            along_z = kz * pltpu.roll(v0, LANES - 1, 1) + pltpu.roll(kz * v0, 1, 1)
            yield i, v0 + q_ref[g, i, here, :] * ((along_x + along_y) + along_z)
            c0, v0, v_before, k_before = c_after, v_after, v0, k_after

    def first(k):
        at = aligned(PAD + 8 * k)
        here, up, down = pl.ds(at, 8), pl.ds(at + 1, 8), pl.ds(at - 1, 8)
        for g in range(groups):
            for i, value in walk(g, d_ref, 2, nxe - 2, here, up, down):
                e_ref[g, i, here, :] = value

    chunks(height // 8, UNROLL[2], first)

    step = 2 if pair else 1
    scale = SCALE * (0.125 if pair else 1.0)
    keep = REST / (SHIFT * SHIFT)

    def second(k):
        at = PAD + EDGE + 8 * k
        here, up, down = pl.ds(at, 8), pl.ds(at + 1, 8), pl.ds(at - 1, 8)
        out = [None] * (nx // step)
        for g in range(groups):
            gain = jnp.broadcast_to(scale * weights[g], (8, LANES))
            held = None
            for i, value in walk(g, e_ref, HALO, nx + HALO, here, up, down):
                value = value + keep * d_ref[g, i, here, :]
                j = i - HALO
                if j % step:
                    value = held + value
                held = value
                if j % step == step - 1:
                    value = gain * value
                    out[j // step] = value if g == 0 else out[j // step] + value
        for j, value in enumerate(out):
            u_ref[j, pl.ds(aligned(8 * k), 8), :] = value

    chunks(ny // 8, UNROLL[3], second)

    out_z = nz // step
    match = iota((out_z, 3 * LANES), 1) % nz // step == iota((out_z, 3 * LANES), 0)
    gather = jnp.where(match, 1.0, 0.0).astype(jnp.bfloat16)
    for j in range(nx // step):
        if pair:
            total = (u_ref[j, pl.ds(0, ny // 2, stride=2), :]
                     + u_ref[j, pl.ds(1, ny // 2, stride=2), :])
        else:
            total = u_ref[j]
        stacked = jnp.concatenate(pieces(total), axis=1)
        finish(j, lax.dot_general(gather, stacked, COLUMNS, preferred_element_type=jnp.float32))


def spread_of(nz):
    match = iota((3 * nz, LANES), 0) % nz == iota((3 * nz, LANES), 1) % nz
    return jnp.where(match, 1.0, 0.0).astype(jnp.bfloat16)


def force_of(source, spread):
    return lax.dot_general(jnp.concatenate(pieces(source), axis=0), spread, ROWS,
                           preferred_element_type=jnp.float32)


def fine_place(here, strip, nx, ny):
    return here.t * strip + here.half * nx, quarter(here.b, here.t, here.tiles) * ny


def table_kernel(tiles, fine_sizes, coarse_sizes, mx_ref, my_ref, mz_ref, sf_ref, sc_ref, order_ref,
                 fx_ref, fy_ref, fz_ref, ff_ref, cx_ref, cy_ref, cz_ref, cf_ref,
                 tx_ref, ty_ref, own_ref, sem):
    here = Place(tiles)
    nx, ny, nz, full_x, full_y = fine_sizes
    strip = sf_ref.shape[0]
    count = nx + REACH
    copy = pltpu.make_async_copy(
        sf_ref.at[pl.ds(jnp.where(here.half == 0, 0, strip - count), count)], own_ref, sem)
    copy.start()
    terms = mx_ref.shape[0]
    tx_ref[...] = jnp.zeros_like(tx_ref)
    tx_ref[0, 0:terms, 0:mx_ref.shape[1]] = mx_ref[...]
    tx_ref[1, 0:terms, 0:mz_ref.shape[1]] = mz_ref[...]
    ty_ref[...] = jnp.zeros_like(ty_ref)
    ty_ref[0:terms, :] = my_ref[...]
    x0, y0 = fine_place(here, strip, nx, ny)
    factors(1, terms, nx, ny, nz, x0, y0, full_x, full_y, tx_ref, ty_ref, fx_ref, fy_ref, fz_ref)
    shift = (EDGE + full_y - y0) % full_y

    nx, ny, nz, full_x, full_y = coarse_sizes
    x0 = here.m * nx
    factors(2, terms, nx, ny, nz, x0, here.t * ny, full_x, full_y, tx_ref, ty_ref,
            cx_ref, cy_ref, cz_ref)
    spread = spread_of(nz)
    for k in range(nx + 2 * REACH):
        x = jnp.clip(x0 - REACH + k, 0, full_x - 1)
        cf_ref[k] = jnp.zeros_like(cf_ref[k])
        cf_ref[k, EDGE:EDGE + ny, :] = force_of(sc_ref[x], spread)

    copy.wait()
    height = ff_ref.shape[1]
    spread = spread_of(fine_sizes[2])

    def place(k):
        source = pltpu.roll(own_ref[k], shift, 1)[:, :height]
        ff_ref[k + REACH * (1 - here.half)] = force_of(source, spread)

    chunks(count, 5 if count % 5 == 0 else 2, place)


def fine_kernel(tiles, groups, sizes, strip, per_device,
                x_ref, y_ref, z_ref, f_ref, one_ref, two_ref, side_ref, order_ref, out_ref,
                yz_ref, c_ref, kz_ref, q_ref, d_ref, e_ref, u_ref, edge_ref):
    here = Place(tiles)
    nx, ny, nz, full_x, full_y = sizes
    height = ny + 2 * EDGE
    x0, y0 = fine_place(here, strip, nx, ny)
    weights = members_of((one_ref, two_ref), groups, nz, 0, per_device, z_ref, yz_ref)
    spread = spread_of(nz)
    for k in range(REACH):
        edge_ref[k] = force_of(side_ref[k * nz:(k + 1) * nz, :height], spread)
    count = nx + REACH

    def force(k, rows):
        if k < REACH:
            return jnp.where(here.half == 0, edge_ref[k, rows, :], f_ref[k, rows, :])
        if k >= count:
            return jnp.where(here.half == 0, f_ref[k, rows, :], edge_ref[k - count, rows, :])
        return f_ref[k, rows, :]

    def finish(j, value):
        out_ref[j] = value

    sweeps(2 * groups, nx, ny, nz, x0, y0, full_x, full_y, True, weights, x_ref, y_ref, yz_ref,
           force, c_ref, kz_ref, q_ref, d_ref, e_ref, u_ref, finish)


def coarse_kernel(tiles, groups, sizes, first_row, per_device,
                  x_ref, y_ref, z_ref, f_ref, par_ref, base_ref, out_ref,
                  yz_ref, c_ref, kz_ref, q_ref, d_ref, e_ref, u_ref):
    here = Place(tiles)
    nx, ny, nz, full_x, full_y = sizes
    weights = members_of((par_ref,), groups, nz, first_row, per_device, z_ref, yz_ref)

    def force(k, rows):
        return f_ref[k, rows, :]

    def finish(j, value):
        out_ref[j] = value if base_ref is None else base_ref[j] + value

    sweeps(groups, nx, ny, nz, here.m * nx, here.t * ny, full_x, full_y, False, weights, x_ref,
           y_ref, yz_ref, force, c_ref, kz_ref, q_ref, d_ref, e_ref, u_ref, finish)


def coarse_near_kernel(tiles, groups, sizes, first_row, per_device, side_at,
                       x_ref, y_ref, z_ref, f_ref, par_ref, a_ref, b_ref, out_ref, full_ref,
                       *scratch_refs):
    here = Place(tiles)
    nx, ny, nz, _, _ = sizes
    spread = spread_of(nz)
    per_group = side_at[2]
    for k in range(nx + 2 * REACH):
        full_ref[k] = f_ref[k]
        rows = slice(k % per_group * nz, (k % per_group + 1) * nz)
        found = []
        for ref, at in ((a_ref, side_at[0]), (b_ref, side_at[1])):
            low = at // 16 * 16
            block = force_of(ref[rows, low:low + 16], spread)
            at = at - low + REACH * (k // per_group)
            found.append(block[at:at + REACH])
        full_ref[k, EDGE - REACH:EDGE, :] = jnp.where(here.half == 0, found[0], found[1])
        full_ref[k, EDGE + ny:EDGE + ny + REACH, :] = jnp.where(
            here.half == 0, found[1], found[0])
    coarse_kernel(tiles, groups, sizes, first_row, per_device, x_ref, y_ref, z_ref, full_ref,
                  par_ref, None, out_ref, *scratch_refs)


def scratch(groups, nx, ny, count):
    nxe, height = nx + 2 * HALO, ny + 2 * EDGE
    grid = pltpu.VMEM((groups, nxe, height + 2 * PAD, LANES), jnp.float32)
    return [pltpu.VMEM((groups, TERMS, LANES), jnp.float32), grid, grid, grid, grid, grid,
            pltpu.VMEM((count, ny, LANES), jnp.float32)]


def level_shapes(nx, ny):
    nxe, height = nx + 2 * HALO, ny + 2 * EDGE
    return (jax.ShapeDtypeStruct((nxe, TERMS, LANES), jnp.float32),
            jax.ShapeDtypeStruct((height, 6 * TERMS), jnp.bfloat16),
            jax.ShapeDtypeStruct((TERMS, LANES), jnp.float32),
            jax.ShapeDtypeStruct((nx + 2 * REACH, height, LANES), jnp.float32))


def limit(mebibytes):
    return pltpu.CompilerParams(vmem_limit_bytes=mebibytes << 20)


VMEM = pl.BlockSpec(memory_space=pltpu.VMEM)
SMEM = pl.BlockSpec(memory_space=pltpu.SMEM)
HBM = pl.BlockSpec(memory_space=pl.ANY)


def solution(mesh):
    members, tiles = mesh.shape["member"], mesh.shape["tile"]
    assert members == 2 * tiles and tiles >= 4
    axes = ("member", "tile")
    bits = (tiles // 2, tiles // 4)
    others = [d for d in range(1, tiles) if d not in bits]

    def flat(b, a, t):
        return (b * 2 + a) * tiles + t

    def everywhere(rule):
        return [(flat(b, a, t), flat(*rule(b, a, t)))
                for b in range(tiles) for a in range(2) for t in range(tiles)]

    def beside(bit, outward):
        def rule(b, a, t):
            step = 1 if a ^ (t % 2) else -1
            to = t + (step if outward else -step)
            return b ^ bit, a, to if 0 <= to < tiles else t
        return everywhere(rule)

    def owner(b, a, t):
        return t, a ^ (t % 2), b ^ t ^ (tiles - 1 if t < tiles // 2 else 0)

    def body(node_fine, node_coarse, weight_fine, weight_coarse, mode_x, mode_y, mode_z,
             source_fine, source_coarse):
        strip, nz, full_y = source_fine.shape
        full_cx, cz, cy = source_coarse.shape
        full_x = mode_x.shape[1]
        nx, ny, cx = full_x // members, full_y // tiles, full_cx // members
        n_fine, n_coarse = node_fine.shape[0], node_coarse.shape[0]
        height = ny + 2 * EDGE
        rows = REACH * nz
        width = -(-(height + REACH * 2) // LANES) * LANES
        fine_sizes = nx, ny, nz, full_x, full_y
        coarse_sizes = cx, cy, cz, full_cx, cy * tiles

        side_a, side_b, par = pl.pallas_call(
            functools.partial(prep_kernel, tiles, nx, ny, cx, bits),
            out_shape=(jax.ShapeDtypeStruct((rows + BLOCK, width), jnp.float32),
                       jax.ShapeDtypeStruct((rows + BLOCK, LANES), jnp.float32),
                       jax.ShapeDtypeStruct((BLOCK, LANES), jnp.float32)),
            in_specs=[VMEM, VMEM, SMEM, SMEM, HBM, VMEM],
            out_specs=(VMEM, VMEM, VMEM),
            scratch_shapes=[pltpu.VMEM((REACH, nz, full_y), jnp.float32), pltpu.SemaphoreType.DMA],
            compiler_params=limit(4),
            name="prep",
        )(node_fine, node_coarse, weight_fine, weight_coarse, source_fine, source_coarse)

        made = pl.pallas_call(
            functools.partial(table_kernel, tiles, fine_sizes, coarse_sizes),
            out_shape=level_shapes(nx, ny) + level_shapes(cx, cy),
            in_specs=[VMEM] * 3 + [HBM, VMEM, HBM],
            out_specs=(VMEM,) * 8,
            scratch_shapes=[pltpu.VMEM((2, TERMS, LANES), jnp.float32),
                            pltpu.VMEM((TERMS, full_y), jnp.float32),
                            pltpu.VMEM((nx + REACH, nz, full_y), jnp.float32),
                            pltpu.SemaphoreType.DMA],
            compiler_params=limit(8),
            name="tables",
        )(mode_x, mode_y, mode_z, source_fine, source_coarse, par)
        of_fine, of_coarse = made[:4], made[4:]

        side_a = lax.ppermute(side_a, axes, beside(bits[0], True))
        side_b = lax.ppermute(side_b, axes, beside(bits[1], False))
        more = [lax.ppermute(par, "member", [(i, i ^ (2 * d)) for i in range(members)])
                for d in others]
        par = jnp.concatenate([par, side_a[rows:, :LANES], side_b[rows:]] + more, axis=0)
        twin = lax.ppermute(par, "member", [(i, i ^ 1) for i in range(members)])

        groups = tiles * n_coarse * cz // LANES
        part = jax.ShapeDtypeStruct((cx, cz, cy), jnp.float32)
        near, force = pl.pallas_call(
            functools.partial(coarse_near_kernel, tiles, groups, coarse_sizes, n_fine, n_coarse,
                              (height, EDGE * 2, rows // cz)),
            out_shape=(part, level_shapes(cx, cy)[3]),
            in_specs=[VMEM] * 7,
            out_specs=(VMEM, VMEM),
            scratch_shapes=scratch(groups, cx, cy, cx),
            compiler_params=limit(16),
            name="coarse_near",
        )(*of_coarse, par, side_a, side_b)

        fine_groups = tiles * n_fine * nz // LANES
        fine = pl.pallas_call(
            functools.partial(fine_kernel, tiles, fine_groups, fine_sizes, strip, n_fine),
            out_shape=jax.ShapeDtypeStruct((nx // 2, nz // 2, ny // 2), jnp.float32),
            in_specs=[VMEM] * 7 + [HBM],
            out_specs=VMEM,
            scratch_shapes=scratch(2 * fine_groups, nx, ny, nx // 2)
            + [pltpu.VMEM((REACH, height, LANES), jnp.float32)],
            compiler_params=limit(24),
            name="fine_smooth",
        )(*of_fine, par, twin, side_a, near)
        arrived = lax.ppermute(fine, axes, everywhere(owner))

        far = pl.pallas_call(
            functools.partial(coarse_kernel, tiles, groups, coarse_sizes, n_fine, n_coarse),
            out_shape=part,
            in_specs=[VMEM] * 6,
            out_specs=VMEM,
            scratch_shapes=scratch(groups, cx, cy, cx),
            compiler_params=limit(16),
            name="coarse_far",
        )(*of_coarse[:3], force, twin, near)
        return arrived + far

    return jax.shard_map(
        body,
        mesh=mesh,
        in_specs=(
            P("member", None), P("member", None), P("member"), P("member"),
            P(), P(), P(), P("tile", None, None), P(None, None, "tile"),
        ),
        out_specs=P("member", None, "tile"),
        check_vma=False,
    )
```

time: 195 us -> 32.6 us (0.17)
  local copies, waits for them, and re-layouts: 78.2 us -> 2.88 us
  other arithmetic: 40.5 us -> 0.62 us
  waiting for transfers between devices: 37.3 us -> 4.33 us
  Pallas kernels: 0 us -> 15.3 us
  between operations: 14.4 us -> 0.8 us
  starting transfers between devices: 17.7 us -> 8.42 us
  matrix products: 6.21 us -> 0 us
    reshape x1 -> x0, local copies, waits for them, and re-layouts: 68.4 us -> none  [restrict(): tensor.reshape(tensor.shape[0] // 2, 2, tensor.shape[1] // 2, 2, tensor.s...]
    reduce_scatter x1 -> x0, waiting for transfers between devices: 32.9 us -> none  [body(): return lax.psum_scatter(summed, 'member', scatter_dimension=0, tiled=True)]
    reduce_sum x1 -> x0, other arithmetic: 20.8 us -> none  [restrict(): return blocks.sum(axis=(1, 3, 5)) * 0.125]
    pallas_call x0 -> x5, Pallas kernels: none -> 15.3 us  [the longest x1 6.32 us: body(): pl.pallas_call(functools.partial(fine_kernel, tiles, fine_groups, fine_si...]
    mul x9 -> x0, other arithmetic: 10.2 us -> none  [the longest x2 7.12 us: smooth_deep(): update = fresh * trim_dim(inside, trim_depth, halo_dim)]
    add x3 -> x1, other arithmetic: 7.92 us -> 0.62 us  [body(): return arrived + far]
    dot_general x3 -> x0, matrix products: 6.21 us -> none  [the longest x1 2.55 us: body(): jnp.tensordot(weight_coarse.astype(jnp.float32), coarse_result, axes=1, p...]
    all_to_all x1 -> x0, starting transfers between devices: 4.92 us -> none  [body(): lax.all_to_all(fine_part, 'tile', split_axis=2, concat_axis=0, tiled=True)]
  transfers between devices with their start and end apart: 6 -> 5, of which waited for: 3 -> 3; matrix products, arithmetic and copies ran while one was open for 11% -> 0% of each run, Pallas kernels for 0% -> 24%
where the time goes in v2:
time: 32.6 us; the launch traced here: 32.4 us
  Pallas kernels  15.3 us (47%)
  starting transfers between devices  8.42 us (26%)
  waiting for transfers between devices  4.33 us (13%)
  local copies, waits for them, and re-layouts  2.88 us (9%)
  between operations  0.8 us (2%)
  other arithmetic  0.62 us (2%)
    pallas_call x1, Pallas kernels, body(): pl.pallas_call(functools.partial(fine_kernel, tiles, fine_groups, fine_si...  6.32 us
    ppermute x1, starting transfers between devices, body(): side_b = lax.ppermute(side_b, axes, beside(bits[1], False))  3.52 us
    pallas_call x1, Pallas kernels, body(): pl.pallas_call(functools.partial(coarse_near_kernel, tiles, groups, coars...  3.23 us
    pallas_call x1, Pallas kernels, body(): pl.pallas_call(functools.partial(coarse_kernel, tiles, groups, coarse_siz...  3.14 us
    ppermute x1, starting transfers between devices, body(): side_a = lax.ppermute(side_a, axes, beside(bits[0], True))  3.06 us
    unnamed x20, local copies, waits for them, and re-layouts  2.88 us
    ppermute x1, waiting for transfers between devices, body(): lax.ppermute(par, 'member', [(i, i ^ 2 * d) for i in range(members)])  2.54 us
    pallas_call x1, Pallas kernels, body(): pl.pallas_call(functools.partial(table_kernel, tiles, fine_sizes, coarse_...  1.57 us
  transfers between devices with their start and end apart: 5, of which 3 were waited for; matrix products, arithmetic and copies ran while one was open for 0% of the time, Pallas kernels for 24%

profile of v2, /device:TPU:0, one launch (start us, length us, event | category | flops | bytes accessed | tf_op | source)
XLA Modules:
  0.0 32.4 jit_solution(4508670713545143499)
XLA Ops:
  0.0 0.0 copy-start.9
  0.0 0.0 copy-start.8
  0.7 0.0 copy-done.9
  0.7 0.0 copy-done.8
  0.7 0.0 copy-start
  0.7 1.2 %copy-done = f32[16,32,512]{2,1,0:T(8,128)S(1)} copy-done((f32[16,32,512]{2,1,0:T(8,128)S(1)}, f32[16,32,512]{2,1,0:T(8,128)}, u32[]{:S(2)}) %copy-start) | copy-done | bytes 1048600
  1.9 0.0 copy-start.2
  1.9 0.9 %copy-done.2 = f32[32,16,64]{2,1,0:T(8,128)S(1)} copy-done((f32[32,16,64]{2,1,0:T(8,128)S(1)}, f32[32,16,64]{2,1,0:T(8,128)}, u32[]{:S(2)}) %copy-start.2) | copy-done | bytes 131096
  2.9 0.0 copy-start.7
  2.9 0.7 %copy-done.7 = s32[4,12]{1,0:T(4,128)S(1)} copy-done((s32[4,12]{1,0:T(4,128)S(1)}, s32[4,12]{1,0:T(4,128)}, u32[]{:S(2)}) %copy-start.7) | copy-done | bytes 216
  3.6 0.0 copy-start.1
  3.6 0.0 copy-start.3
  3.6 1.1 %prep.1 = (f32[72,256]{1,0:T(8,128)S(1)}, f32[72,128]{1,0:T(8,128)S(1)}, f32[8,128]{1,0:T(8,128)S(1)}) custom-call(s32[1,12]{1,0:T(1,128)S(1)} %copy-done.8, s32[4,12]{1,0:T(4,128)S(1)} %copy-done.7, s32[1]{0:T(128)S(6)} %copy.10.wf_ref, s32[4]{0:T(128)S(1)} %copy-done.9, f32[16,32,512]{2,1,0:T(8,128)S(1)} %copy-done, f32[32,16,64]{2,1,0:T(8,128)S(1)} %copy-done.2), custom_call_target="tpu_custom_call" | custom-call | tf_op jit(solution)/shard_map/prep/pallas_call | solution.py:506
  4.6 0.0 copy-start.4
  4.6 3.1 %collective-permute-start = (f32[72,256]{1,0:T(8,128)S(1)}, f32[72,256]{1,0:T(8,128)S(1)}, u32[]{:S(2)}, u32[]{:S(2)}) collective-permute-start(f32[72,256]{1,0:T(8,128)S(1)} %get-tuple-element.23), channel_id=1, source_target_pairs={{0,16},{1,18},{2,17},{3,19},{4,21},{5,20},{6,23},{7,22},{8,24},{9,... | collective-permute-start | bytes 221192 | tf_op jit(solution)/shard_map/ppermute | solution.py:532
  7.7 3.5 %collective-permute-start.1 = (f32[72,128]{1,0:T(8,128)S(1)}, f32[72,128]{1,0:T(8,128)S(1)}, u32[]{:S(2)}, u32[]{:S(2)}) collective-permute-start(f32[72,128]{1,0:T(8,128)S(1)} %get-tuple-element.24), channel_id=1, source_target_pairs={{0,9},{1,8},{2,11},{3,10},{4,12},{5,14},{6,13},{7,15},{8,1},{9,0},... | collective-permute-start | bytes 110600 | tf_op jit(solution)/shard_map/ppermute | solution.py:533
  11.2 0.5 %collective-permute-start.2 = (f32[8,128]{1,0:T(8,128)S(1)}, f32[8,128]{1,0:T(8,128)S(1)}, u32[]{:S(2)}, u32[]{:S(2)}) collective-permute-start(f32[8,128]{1,0:T(8,128)S(1)} %get-tuple-element.18.order_ref), channel_id=1, source_target_pairs={{0,24},{4,28},{8,16},{12,20},{16,8},{20,12},{24,0},{28,4},{1,25},{... | collective-permute-start | bytes 12296 | tf_op jit(solution)/shard_map/ppermute | solution.py:534
  11.7 1.5 %collective-permute-done.1.b_ref = f32[72,128]{1,0:T(8,128)S(1)} collective-permute-done((f32[72,128]{1,0:T(8,128)S(1)}, f32[72,128]{1,0:T(8,128)S(1)}, u32[]{:S(2)}, u32[]{:S(2)}) %collective-permute-start.1) | collective-permute-done | bytes 36896 | tf_op jit(solution)/shard_map/ppermute | solution.py:533
  13.2 0.0 collective-permute-done.a_ref.side_ref
  13.2 0.0 copy-start.5
  13.2 0.0 copy-start.6
  13.2 2.5 %collective-permute-done.2 = f32[8,128]{1,0:T(8,128)S(1)} collective-permute-done((f32[8,128]{1,0:T(8,128)S(1)}, f32[8,128]{1,0:T(8,128)S(1)}, u32[]{:S(2)}, u32[]{:S(2)}) %collective-permute-start.2) | collective-permute-done | bytes 4128 | tf_op jit(solution)/shard_map/ppermute | solution.py:534
  15.7 0.0 collective-permute-start.3
  15.7 0.0 copy-done.1
  15.7 0.0 copy-done.3
  15.8 0.0 copy-done.4
  15.8 0.0 copy-done.5
  15.8 0.0 copy-done.6
  15.8 1.6 %tables.1 = (f32[14,16,128]{2,1,0:T(8,128)S(1)}, bf16[136,96]{1,0:T(8,128)(2,1)S(1)}, f32[16,128]{1,0:T(8,128)S(1)}, f32[12,136,128]{2,1,0:T(8,128)S(1)}, f32[10...) custom-call(f32[12,64]{1,0:T(8,128)S(1)} %copy-done.5, ...), custom_call_target="tpu_custom_call" | custom-call | tf_op jit(solution)/shard_map/tables/pallas_call | solution.py:518
  17.4 3.2 %coarse_near.1 = (f32[4,16,64]{2,1,0:T(8,128)S(1)}, f32[8,72,128]{2,1,0:T(8,128)S(1)}) custom-call(f32[10,16,128]{2,1,0:T(8,128)S(1)} %get-tuple-element.25.x_ref, bf16[72,96]{1,0:T(8,128)(2,1)S(1)} %get-tuple-element.26.y_ref, f32[16,128]{1,0:T(8,128)S(1)} %get-tuple-element.27.z_ref, f32[8,72,128]{2,1,0:T(8,128)S(1)} %get-tuple-element.28.f_ref, ...), custom_call_target="tpu_custom_call" | custom-call | tf_op jit(solution)/shard_map/coarse_near/pallas_call | solution.py:541
  20.6 0.0 collective-permute-done.3.two_ref.par_ref
  20.6 6.3 %fine_smooth.1 = f32[4,16,64]{2,1,0:T(8,128)S(1)} custom-call(f32[14,16,128]{2,1,0:T(8,128)S(1)} %get-tuple-element.19.x_ref, bf16[136,96]{1,0:T(8,128)(2,1)S(1)} %get-tuple-element.20.y_ref, f32[16,128]{1,0:T(8,128)S(1)} %get-tuple-element.21.z_ref, f32[12,136,128]{2,1,0:T(8,128)S(1)} %get-tuple-element.22.f_ref, ...), custom_call_target="tpu_custom_call" | custom-call | tf_op jit(solution)/shard_map/fine_smooth/pallas_call | solution.py:553
  26.9 1.4 %collective-permute-start.4 = (f32[4,16,64]{2,1,0:T(8,128)S(1)}, f32[4,16,64]{2,1,0:T(8,128)S(1)}, u32[]{:S(2)}, u32[]{:S(2)}) collective-permute-start(f32[4,16,64]{2,1,0:T(8,128)S(1)} %fine_smooth.1), channel_id=1, source_target_pairs={{0,3},{1,14},{2,18},{3,31},{4,7},{5,10},{6,22},{7,27},{8,2},{9,15}... | collective-permute-start | bytes 49160 | tf_op jit(solution)/shard_map/ppermute | solution.py:563
  28.3 3.1 %coarse_far.1 = f32[4,16,64]{2,1,0:T(8,128)S(1)} custom-call(f32[10,16,128]{2,1,0:T(8,128)S(1)} %get-tuple-element.25.x_ref, bf16[72,96]{1,0:T(8,128)(2,1)S(1)} %get-tuple-element.26.y_ref, f32[16,128]{1,0:T(8,128)S(1)} %get-tuple-element.27.z_ref, f32[8,72,128]{2,1,0:T(8,128)S(1)} %get-tuple-element.30.f_ref, ...), custom_call_target="tpu_custom_call" | custom-call | tf_op jit(solution)/shard_map/coarse_far/pallas_call | solution.py:565
  31.4 0.3 collective-permute-done.4
  31.7 0.6 %add.3 = f32[4,16,64]{2,1,0:T(8,128)} add(f32[4,16,64]{2,1,0:T(8,128)S(1)} %collective-permute-done.4, f32[4,16,64]{2,1,0:T(8,128)S(1)} %coarse_far.1) | non-fusion elementwise | flops 4096 | bytes 49152 | tf_op jit(solution)/shard_map/add | solution.py:574
  (3 shorter events, 0.0 us)
Async XLA Ops:
  0.0 0.7 %copy-start.9 = (s32[4]{0:T(128)S(1)}, s32[4]{0:T(128)}, u32[]{:S(2)}) copy-start(s32[4]{0:T(128)} %wc_ref.1) | copy-start | bytes 52
  0.0 0.7 %copy-start.8 = (s32[1,12]{1,0:T(1,128)S(1)}, s32[1,12]{1,0:T(1,128)}, u32[]{:S(2)}) copy-start(s32[1,12]{1,0:T(1,128)} %nf_ref.1) | copy-start | bytes 148
  0.7 1.2 %copy-start = (f32[16,32,512]{2,1,0:T(8,128)S(1)}, f32[16,32,512]{2,1,0:T(8,128)}, u32[]{:S(2)}) copy-start(f32[16,32,512]{2,1,0:T(8,128)} %sf_ref.3) | copy-start | bytes 3145732
  1.9 0.9 %copy-start.2 = (f32[32,16,64]{2,1,0:T(8,128)S(1)}, f32[32,16,64]{2,1,0:T(8,128)}, u32[]{:S(2)}) copy-start(f32[32,16,64]{2,1,0:T(8,128)} %sc_ref.3) | copy-start | bytes 393220
  2.9 0.7 %copy-start.7 = (s32[4,12]{1,0:T(4,128)S(1)}, s32[4,12]{1,0:T(4,128)}, u32[]{:S(2)}) copy-start(s32[4,12]{1,0:T(4,128)} %nc_ref.1) | copy-start | bytes 580
  3.6 12.2 %copy-start.1 = (f32[16,32,512]{2,1,0:T(8,128)S(1)}, f32[16,32,512]{2,1,0:T(8,128)}, u32[]{:S(2)}) copy-start(f32[16,32,512]{2,1,0:T(8,128)} %sf_ref.3) | copy-start | bytes 3145732
  3.6 12.2 %copy-start.3 = (f32[32,16,64]{2,1,0:T(8,128)S(1)}, f32[32,16,64]{2,1,0:T(8,128)}, u32[]{:S(2)}) copy-start(f32[32,16,64]{2,1,0:T(8,128)} %sc_ref.3) | copy-start | bytes 393220
  4.6 11.1 %copy-start.4 = (f32[12,512]{1,0:T(8,128)S(1)}, f32[12,512]{1,0:T(8,128)}, u32[]{:S(2)}) copy-start(f32[12,512]{1,0:T(8,128)} %my_ref.1) | copy-start | bytes 73732
  4.6 8.5 %collective-permute-start = (f32[72,256]{1,0:T(8,128)S(1)}, f32[72,256]{1,0:T(8,128)S(1)}, u32[]{:S(2)}, u32[]{:S(2)}) collective-permute-start(f32[72,256]{1,0:T(8,128)S(1)} %get-tuple-element.23), channel_id=1, source_target_pairs={{0,16},{1,18},{2,17},{3,19},{4,21},{5,20},{6,23},{7,22},{8,24},{9,... | collective-permute-start | bytes 221192 | tf_op jit(solution)/shard_map/ppermute | solution.py:532
  7.7 5.5 %collective-permute-start.1 = (f32[72,128]{1,0:T(8,128)S(1)}, f32[72,128]{1,0:T(8,128)S(1)}, u32[]{:S(2)}, u32[]{:S(2)}) collective-permute-start(f32[72,128]{1,0:T(8,128)S(1)} %get-tuple-element.24), channel_id=1, source_target_pairs={{0,9},{1,8},{2,11},{3,10},{4,12},{5,14},{6,13},{7,15},{8,1},{9,0},... | collective-permute-start | bytes 110600 | tf_op jit(solution)/shard_map/ppermute | solution.py:533
  11.2 4.5 %collective-permute-start.2 = (f32[8,128]{1,0:T(8,128)S(1)}, f32[8,128]{1,0:T(8,128)S(1)}, u32[]{:S(2)}, u32[]{:S(2)}) collective-permute-start(f32[8,128]{1,0:T(8,128)S(1)} %get-tuple-element.18.order_ref), channel_id=1, source_target_pairs={{0,24},{4,28},{8,16},{12,20},{16,8},{20,12},{24,0},{28,4},{1,25},{... | collective-permute-start | bytes 12296 | tf_op jit(solution)/shard_map/ppermute | solution.py:534
  13.2 2.6 %copy-start.5 = (f32[12,64]{1,0:T(8,128)S(1)}, f32[12,64]{1,0:T(8,128)}, u32[]{:S(2)}) copy-start(f32[12,64]{1,0:T(8,128)} %mx_ref.1) | copy-start | bytes 9220
  13.2 2.6 %copy-start.6 = (f32[12,32]{1,0:T(8,128)S(1)}, f32[12,32]{1,0:T(8,128)}, u32[]{:S(2)}) copy-start(f32[12,32]{1,0:T(8,128)} %mz_ref.1) | copy-start | bytes 4612
  15.7 4.9 %collective-permute-start.3 = (f32[32,128]{1,0:T(8,128)S(1)}, f32[32,128]{1,0:T(8,128)S(1)}, u32[]{:S(2)}, u32[]{:S(2)}) collective-permute-start(f32[32,128]{1,0:T(8,128)S(1)} %pad_maximum_fusion.par_ref.one_ref), channel_id=1, source_target_pairs={{0,4},{4,0},{8,12},{12,8},{16,20},{20,16},{24,28},{28,24},{1,5},{5... | collective-permute-start | bytes 49160 | tf_op jit(solution)/shard_map/ppermute | solution.py:537
  26.9 4.8 %collective-permute-start.4 = (f32[4,16,64]{2,1,0:T(8,128)S(1)}, f32[4,16,64]{2,1,0:T(8,128)S(1)}, u32[]{:S(2)}, u32[]{:S(2)}) collective-permute-start(f32[4,16,64]{2,1,0:T(8,128)S(1)} %fine_smooth.1), channel_id=1, source_target_pairs={{0,3},{1,14},{2,18},{3,31},{4,7},{5,10},{6,22},{7,27},{8,2},{9,15}... | collective-permute-start | bytes 49160 | tf_op jit(solution)/shard_map/ppermute | solution.py:563

commit v3 on v2

--- a/solution.py
+++ b/solution.py
@@ -22,7 +22,6 @@
 FAR = -2048.0
 TERMS = 16
 BLOCK = 8
-UNROLL = (2, 2, 2, 2)
 
 
 def sweep_factors(sweep_count):
@@ -80,15 +79,25 @@
         return jnp.where((to >= 0) & (to < self.tiles), to, self.t)
 
 
-def prep_kernel(tiles, nx, ny, cx, bits, nf_ref, nc_ref, wf_ref, wc_ref, sf_ref, sc_ref,
-                a_ref, b_ref, par_ref, plane_ref, sem):
+def prep_kernel(tiles, nx, ny, cx, bits, nf_hbm, nc_hbm, wf_ref, wc_ref, sf_ref, sc_hbm,
+                a_ref, b_ref, par_ref, plane_ref, nf_ref, nc_ref, sc_ref, sems):
     here = Place(tiles)
     strip, nz, full_y = sf_ref.shape
-    full_x, cz, cy = sc_ref.shape
+    full_x, cz, cy = sc_hbm.shape
     height = ny + 2 * EDGE
     start = jnp.where(here.half == 1, strip - REACH, 0)
-    copy = pltpu.make_async_copy(sf_ref.at[pl.ds(start, REACH)], plane_ref, sem)
+    copy = pltpu.make_async_copy(sf_ref.at[pl.ds(start, REACH)], plane_ref, sems.at[0])
     copy.start()
+    window = cx + 2 * REACH
+    lows = [jnp.clip(cx * ((here.b ^ bit) * 2 + here.a) - REACH, 0, full_x - window) for bit in bits]
+    blocks = [pltpu.make_async_copy(sc_hbm.at[pl.ds(lows[k], window)], sc_ref.at[k], sems.at[3 + k])
+              for k in range(2)]
+    nodes = [pltpu.make_async_copy(nf_hbm, nf_ref, sems.at[1]),
+             pltpu.make_async_copy(nc_hbm, nc_ref, sems.at[2])]
+    for item in nodes + blocks:
+        item.start()
+    for item in nodes:
+        item.wait()
 
     def node_values(ref):
         nodes = ref[...]
@@ -112,11 +121,14 @@
     per_group = rows // cz
     spot = iota((rows, LANES), 1)
 
-    def coarse_side(to_b, last, at):
-        first = cx * (to_b * 2 + here.a) - REACH
+    for item in blocks:
+        item.wait()
+
+    def coarse_side(side, last, at):
+        shifted = cx * ((here.b ^ bits[side]) * 2 + here.a) - REACH - lows[side]
         total = jnp.zeros((rows, LANES), jnp.float32)
         for group in range((cx + 2 * REACH) // per_group):
-            parts = [sc_ref[jnp.clip(first + group * per_group + k, 0, full_x - 1)]
+            parts = [sc_ref[side, jnp.clip(shifted + group * per_group + k, 0, window - 1)]
                      for k in range(per_group)]
             block = jnp.concatenate(parts, axis=0)
             block = jnp.concatenate([block] * (LANES // cy), axis=1)
@@ -126,8 +138,8 @@
             total = jnp.where((spot >= to) & (spot < to + REACH), block, total)
         return total
 
-    b_ref[0:rows, :] = coarse_side(here.b ^ bits[1], here.half == 0, EDGE * 2)
-    edge = coarse_side(here.b ^ bits[0], here.half == 1, height % LANES)
+    b_ref[0:rows, :] = coarse_side(1, here.half == 0, EDGE * 2)
+    edge = coarse_side(0, here.half == 1, height % LANES)
     b_ref[rows:rows + BLOCK, :] = par_ref[...]
     a_ref[rows:rows + BLOCK, 0:LANES] = par_ref[...]
 
@@ -189,15 +201,8 @@
     return weights
 
 
-def chunks(count, size, run):
-    def step(j, carry):
-        for s in range(size):
-            run(size * j + s)
-        return carry
-
-    whole = count // size
-    lax.fori_loop(0, whole, step, 0)
-    for k in range(whole * size, count):
+def chunks(count, run):
+    for k in range(count):
         run(k)
 
 
@@ -214,7 +219,7 @@
             c_ref[g, i, pl.ds(PAD, height), :] = jnp.exp(power)
         return carry
 
-    lax.fori_loop(0, nxe, conduct, 0, unroll=UNROLL[0])
+    lax.fori_loop(0, nxe, conduct, 0, unroll=nxe)
 
     lane = iota((8, LANES), 1) % nz
     is_last, is_first = lane == nz - 1, lane == 0
@@ -237,7 +242,7 @@
                 kz_ref[g, i, here, :] = jnp.where(is_last, 0.0, c0 + zp)
                 before, c0 = c0, after
 
-    chunks(height // 8, UNROLL[1], start)
+    chunks(height // 8, start)
 
     def clear_planes(planes):
         for g in range(groups):
@@ -280,7 +285,7 @@
             for i, value in walk(g, d_ref, 2, nxe - 2, here, up, down):
                 e_ref[g, i, here, :] = value
 
-    chunks(height // 8, UNROLL[2], first)
+    chunks(height // 8, first)
 
     step = 2 if pair else 1
     scale = SCALE * (0.125 if pair else 1.0)
@@ -305,7 +310,7 @@
         for j, value in enumerate(out):
             u_ref[j, pl.ds(aligned(8 * k), 8), :] = value
 
-    chunks(ny // 8, UNROLL[3], second)
+    chunks(ny // 8, second)
 
     out_z = nz // step
     match = iota((out_z, 3 * LANES), 1) % nz // step == iota((out_z, 3 * LANES), 0)
@@ -372,7 +377,7 @@
         source = pltpu.roll(own_ref[k], shift, 1)[:, :height]
         ff_ref[k + REACH * (1 - here.half)] = force_of(source, spread)
 
-    chunks(count, 5 if count % 5 == 0 else 2, place)
+    chunks(count, place)
 
 
 def fine_kernel(tiles, groups, sizes, strip, per_device,
@@ -464,6 +469,7 @@
 VMEM = pl.BlockSpec(memory_space=pltpu.VMEM)
 SMEM = pl.BlockSpec(memory_space=pltpu.SMEM)
 HBM = pl.BlockSpec(memory_space=pl.ANY)
+FIXED = pl.BlockSpec(memory_space=pltpu.HBM)
 
 
 def solution(mesh):
@@ -508,10 +514,14 @@
             out_shape=(jax.ShapeDtypeStruct((rows + BLOCK, width), jnp.float32),
                        jax.ShapeDtypeStruct((rows + BLOCK, LANES), jnp.float32),
                        jax.ShapeDtypeStruct((BLOCK, LANES), jnp.float32)),
-            in_specs=[VMEM, VMEM, SMEM, SMEM, HBM, VMEM],
+            in_specs=[FIXED, FIXED, SMEM, SMEM, FIXED, FIXED],
             out_specs=(VMEM, VMEM, VMEM),
-            scratch_shapes=[pltpu.VMEM((REACH, nz, full_y), jnp.float32), pltpu.SemaphoreType.DMA],
-            compiler_params=limit(4),
+            scratch_shapes=[pltpu.VMEM((REACH, nz, full_y), jnp.float32),
+                            pltpu.VMEM(node_fine.shape, jnp.int32),
+                            pltpu.VMEM(node_coarse.shape, jnp.int32),
+                            pltpu.VMEM((2, cx + 2 * REACH, cz, cy), jnp.float32),
+                            pltpu.SemaphoreType.DMA((5,))],
+            compiler_params=pltpu.CompilerParams(vmem_limit_bytes=67043328 - (200 << 10)),
             name="prep",
         )(node_fine, node_coarse, weight_fine, weight_coarse, source_fine, source_coarse)
 
@@ -527,12 +537,13 @@
             compiler_params=limit(8),
             name="tables",
         )(mode_x, mode_y, mode_z, source_fine, source_coarse, par)
-        of_fine, of_coarse = made[:4], made[4:]
 
         side_a = lax.ppermute(side_a, axes, beside(bits[0], True))
         side_b = lax.ppermute(side_b, axes, beside(bits[1], False))
         more = [lax.ppermute(par, "member", [(i, i ^ (2 * d)) for i in range(members)])
                 for d in others]
+        par, made = lax.optimization_barrier((par, made))
+        of_fine, of_coarse = made[:4], made[4:]
         par = jnp.concatenate([par, side_a[rows:, :LANES], side_b[rows:]] + more, axis=0)
         twin = lax.ppermute(par, "member", [(i, i ^ 1) for i in range(members)])
 

time: 32.6 us -> 25.1 us (0.77)
  Pallas kernels: 15.3 us -> 10.6 us
  waiting for transfers between devices: 4.33 us -> 2.29 us
  local copies, waits for them, and re-layouts: 2.88 us -> 2.19 us
    pallas_call x1, Pallas kernels: 6.32 us -> 3.26 us  [body(): pl.pallas_call(functools.partial(fine_kernel, tiles, fine_groups, fine_si...]
    ppermute x1, waiting for transfers between devices: 2.54 us -> 0.31 us  [body(): lax.ppermute(par, 'member', [(i, i ^ 2 * d) for i in range(members)])]
    pallas_call x1, Pallas kernels: 1.06 us -> 2.74 us  [body(): pl.pallas_call(functools.partial(prep_kernel, tiles, nx, ny, cx, bits), o...]
    ppermute x1, waiting for transfers between devices: 0.32 us -> 1.97 us  [body(): arrived = lax.ppermute(fine, axes, everywhere(owner))]
    pallas_call x1, Pallas kernels: 3.14 us -> 1.49 us  [body(): pl.pallas_call(functools.partial(coarse_kernel, tiles, groups, coarse_siz...]
    pallas_call x1, Pallas kernels: 3.23 us -> 1.6 us  [body(): pl.pallas_call(functools.partial(coarse_near_kernel, tiles, groups, coars...]
    ppermute x1, waiting for transfers between devices: 1.46 us -> 0.01 us  [body(): side_b = lax.ppermute(side_b, axes, beside(bits[1], False))]
    unnamed x20 -> x12, local copies, waits for them, and re-layouts: 2.88 us -> 2.19 us
  transfers between devices with their start and end apart: 5 -> 5, of which waited for: 3 -> 2; matrix products, arithmetic and copies ran while one was open for 0% -> 0% of each run, Pallas kernels for 24% -> 18%
where the time goes in v3:
time: 25.1 us; the launch traced here: 24.8 us
  Pallas kernels  10.6 us (42%)
  starting transfers between devices  8.42 us (34%)
  waiting for transfers between devices  2.29 us (9%)
  local copies, waits for them, and re-layouts  2.19 us (9%)
  between operations  0.75 us (3%)
  other arithmetic  0.62 us (2%)
    ppermute x1, starting transfers between devices, body(): side_b = lax.ppermute(side_b, axes, beside(bits[1], False))  3.52 us
    pallas_call x1, Pallas kernels, body(): pl.pallas_call(functools.partial(fine_kernel, tiles, fine_groups, fine_si...  3.26 us
    ppermute x1, starting transfers between devices, body(): side_a = lax.ppermute(side_a, axes, beside(bits[0], True))  3.06 us
    pallas_call x1, Pallas kernels, body(): pl.pallas_call(functools.partial(prep_kernel, tiles, nx, ny, cx, bits), o...  2.74 us
    unnamed x12, local copies, waits for them, and re-layouts  2.19 us
    ppermute x1, waiting for transfers between devices, body(): arrived = lax.ppermute(fine, axes, everywhere(owner))  1.97 us
    pallas_call x1, Pallas kernels, body(): pl.pallas_call(functools.partial(coarse_near_kernel, tiles, groups, coars...  1.6 us
    pallas_call x1, Pallas kernels, body(): pl.pallas_call(functools.partial(coarse_kernel, tiles, groups, coarse_siz...  1.49 us
  transfers between devices with their start and end apart: 5, of which 2 were waited for; matrix products, arithmetic and copies ran while one was open for 0% of the time, Pallas kernels for 18%

profile of v3, /device:TPU:0, one launch (start us, length us, event | category | flops | bytes accessed | tf_op | source)
XLA Modules:
  0.0 24.8 jit_solution(6745084890242531301)
XLA Ops:
  0.7 0.0 copy-start.2
  0.7 0.0 copy-start.4
  0.7 0.0 copy-start.5
  0.7 2.7 %prep.1 = (f32[72,256]{1,0:T(8,128)}, f32[72,128]{1,0:T(8,128)}, f32[8,128]{1,0:T(8,128)}) custom-call(s32[1,12]{1,0:T(1,128)} %nf_hbm.1, s32[4,12]{1,0:T(4,128)} %nc_hbm.1, s32[1]{0:T(128)S(6)} %copy.10.wf_ref, s32[4]{0:T(128)} %wc_ref.1, f32[16,32,512]{2,1,0:T(8,128)} %sf_ref.3, f32[32,16,64]{2,1,0:T(8,128)} %sc_ref.1), custom_call_target="tpu_custom_call" | custom-call | tf_op jit(solution)/shard_map/prep/pallas_call | solution.py:512
  3.4 0.0 copy-start.3
  3.4 3.1 %collective-permute-start = (f32[72,256]{1,0:T(8,128)}, f32[72,256]{1,0:T(8,128)S(1)}, u32[]{:S(2)}, u32[]{:S(2)}) collective-permute-start(f32[72,256]{1,0:T(8,128)} %get-tuple-element.41), channel_id=1, source_target_pairs={{0,16},{1,18},{2,17},{3,19},{4,21},{5,20},{6,23},{7,22},{8,24},{9,... | collective-permute-start | bytes 221192 | tf_op jit(solution)/shard_map/ppermute | solution.py:541
  6.5 3.5 %collective-permute-start.1 = (f32[72,128]{1,0:T(8,128)}, f32[72,128]{1,0:T(8,128)S(1)}, u32[]{:S(2)}, u32[]{:S(2)}) collective-permute-start(f32[72,128]{1,0:T(8,128)} %get-tuple-element.42), channel_id=1, source_target_pairs={{0,9},{1,8},{2,11},{3,10},{4,12},{5,14},{6,13},{7,15},{8,1},{9,0},... | collective-permute-start | bytes 110600 | tf_op jit(solution)/shard_map/ppermute | solution.py:542
  10.0 0.0 copy-done.3
  10.0 0.5 %collective-permute-start.2 = (f32[8,128]{1,0:T(8,128)S(1)}, f32[8,128]{1,0:T(8,128)S(1)}, u32[]{:S(2)}, u32[]{:S(2)}) collective-permute-start(f32[8,128]{1,0:T(8,128)S(1)} %copy-done.3), channel_id=1, source_target_pairs={{0,24},{4,28},{8,16},{12,20},{16,8},{20,12},{24,0},{28,4},{1,25},{... | collective-permute-start | bytes 12296 | tf_op jit(solution)/shard_map/ppermute | solution.py:543
  10.5 0.0 copy-done.2
  10.5 0.0 copy-done.4
  10.5 0.0 copy-done.5
  10.5 0.0 copy-start
  10.5 1.2 %copy-done = f32[16,32,512]{2,1,0:T(8,128)S(1)} copy-done((f32[16,32,512]{2,1,0:T(8,128)S(1)}, f32[16,32,512]{2,1,0:T(8,128)}, u32[]{:S(2)}) %copy-start) | copy-done | bytes 1048600
  11.7 0.0 copy-start.1
  11.7 0.9 %copy-done.1 = f32[32,16,64]{2,1,0:T(8,128)S(1)} copy-done((f32[32,16,64]{2,1,0:T(8,128)S(1)}, f32[32,16,64]{2,1,0:T(8,128)}, u32[]{:S(2)}) %copy-start.1) | copy-done | bytes 131096
  12.7 1.5 %tables.1 = (f32[14,16,128]{2,1,0:T(8,128)S(1)}, bf16[136,96]{1,0:T(8,128)(2,1)S(1)}, f32[16,128]{1,0:T(8,128)S(1)}, f32[12,136,128]{2,1,0:T(8,128)S(1)}, f32[10...) custom-call(f32[12,64]{1,0:T(8,128)S(1)} %copy-done.4, ...), custom_call_target="tpu_custom_call" | custom-call | tf_op jit(solution)/shard_map/tables/pallas_call | solution.py:528
  14.2 0.0 collective-permute-done.1.b_ref
  14.2 0.0 collective-permute-done.a_ref.side_ref
  14.2 0.3 %collective-permute-done.2 = f32[8,128]{1,0:T(8,128)S(1)} collective-permute-done((f32[8,128]{1,0:T(8,128)S(1)}, f32[8,128]{1,0:T(8,128)S(1)}, u32[]{:S(2)}, u32[]{:S(2)}) %collective-permute-start.2) | collective-permute-done | bytes 4128 | tf_op jit(solution)/shard_map/ppermute | solution.py:543
  14.5 0.0 collective-permute-start.3
  14.5 1.6 %coarse_near.1 = (f32[4,16,64]{2,1,0:T(8,128)S(1)}, f32[8,72,128]{2,1,0:T(8,128)S(1)}) custom-call(f32[10,16,128]{2,1,0:T(8,128)S(1)} %get-tuple-element.43.x_ref, bf16[72,96]{1,0:T(8,128)(2,1)S(1)} %get-tuple-element.44.y_ref, f32[16,128]{1,0:T(8,128)S(1)} %get-tuple-element.45.z_ref, f32[8,72,128]{2,1,0:T(8,128)S(1)} %get-tuple-element.46.f_ref, ...), custom_call_target="tpu_custom_call" | custom-call | tf_op jit(solution)/shard_map/coarse_near/pallas_call | solution.py:552
  16.1 0.0 collective-permute-done.3.two_ref.par_ref
  16.1 3.3 %fine_smooth.1 = f32[4,16,64]{2,1,0:T(8,128)S(1)} custom-call(f32[14,16,128]{2,1,0:T(8,128)S(1)} %get-tuple-element.36.x_ref, bf16[136,96]{1,0:T(8,128)(2,1)S(1)} %get-tuple-element.37.y_ref, f32[16,128]{1,0:T(8,128)S(1)} %get-tuple-element.38.z_ref, f32[12,136,128]{2,1,0:T(8,128)S(1)} %get-tuple-element.39.f_ref, ...), custom_call_target="tpu_custom_call" | custom-call | tf_op jit(solution)/shard_map/fine_smooth/pallas_call | solution.py:564
  19.4 1.4 %collective-permute-start.4 = (f32[4,16,64]{2,1,0:T(8,128)S(1)}, f32[4,16,64]{2,1,0:T(8,128)S(1)}, u32[]{:S(2)}, u32[]{:S(2)}) collective-permute-start(f32[4,16,64]{2,1,0:T(8,128)S(1)} %fine_smooth.1), channel_id=1, source_target_pairs={{0,3},{1,14},{2,18},{3,31},{4,7},{5,10},{6,22},{7,27},{8,2},{9,15}... | collective-permute-start | bytes 49160 | tf_op jit(solution)/shard_map/ppermute | solution.py:574
  20.8 1.5 %coarse_far.1 = f32[4,16,64]{2,1,0:T(8,128)S(1)} custom-call(f32[10,16,128]{2,1,0:T(8,128)S(1)} %get-tuple-element.43.x_ref, bf16[72,96]{1,0:T(8,128)(2,1)S(1)} %get-tuple-element.44.y_ref, f32[16,128]{1,0:T(8,128)S(1)} %get-tuple-element.45.z_ref, f32[8,72,128]{2,1,0:T(8,128)S(1)} %get-tuple-element.48.f_ref, ...), custom_call_target="tpu_custom_call" | custom-call | tf_op jit(solution)/shard_map/coarse_far/pallas_call | solution.py:576
  22.3 2.0 %collective-permute-done.4 = f32[4,16,64]{2,1,0:T(8,128)S(1)} collective-permute-done((f32[4,16,64]{2,1,0:T(8,128)S(1)}, f32[4,16,64]{2,1,0:T(8,128)S(1)}, u32[]{:S(2)}, u32[]{:S(2)}) %collective-permute-start.4) | collective-permute-done | bytes 16416 | tf_op jit(solution)/shard_map/ppermute | solution.py:574
  24.2 0.6 %add.3 = f32[4,16,64]{2,1,0:T(8,128)} add(f32[4,16,64]{2,1,0:T(8,128)S(1)} %collective-permute-done.4, f32[4,16,64]{2,1,0:T(8,128)S(1)} %coarse_far.1) | non-fusion elementwise | flops 4096 | bytes 49152 | tf_op jit(solution)/shard_map/add | solution.py:585
  (3 shorter events, 0.0 us)
Async XLA Ops:
  0.7 9.8 %copy-start.2 = (f32[12,512]{1,0:T(8,128)S(1)}, f32[12,512]{1,0:T(8,128)}, u32[]{:S(2)}) copy-start(f32[12,512]{1,0:T(8,128)} %my_ref.1) | copy-start | bytes 73732
  0.7 9.8 %copy-start.4 = (f32[12,64]{1,0:T(8,128)S(1)}, f32[12,64]{1,0:T(8,128)}, u32[]{:S(2)}) copy-start(f32[12,64]{1,0:T(8,128)} %mx_ref.1) | copy-start | bytes 9220
  0.7 9.8 %copy-start.5 = (f32[12,32]{1,0:T(8,128)S(1)}, f32[12,32]{1,0:T(8,128)}, u32[]{:S(2)}) copy-start(f32[12,32]{1,0:T(8,128)} %mz_ref.1) | copy-start | bytes 4612
  3.4 6.6 %copy-start.3 = (f32[8,128]{1,0:T(8,128)S(1)}, f32[8,128]{1,0:T(8,128)}, u32[]{:S(2)}) copy-start(f32[8,128]{1,0:T(8,128)} %get-tuple-element.40.order_ref) | copy-start | bytes 12292
  3.4 10.8 %collective-permute-start = (f32[72,256]{1,0:T(8,128)}, f32[72,256]{1,0:T(8,128)S(1)}, u32[]{:S(2)}, u32[]{:S(2)}) collective-permute-start(f32[72,256]{1,0:T(8,128)} %get-tuple-element.41), channel_id=1, source_target_pairs={{0,16},{1,18},{2,17},{3,19},{4,21},{5,20},{6,23},{7,22},{8,24},{9,... | collective-permute-start | bytes 221192 | tf_op jit(solution)/shard_map/ppermute | solution.py:541
  6.5 7.7 %collective-permute-start.1 = (f32[72,128]{1,0:T(8,128)}, f32[72,128]{1,0:T(8,128)S(1)}, u32[]{:S(2)}, u32[]{:S(2)}) collective-permute-start(f32[72,128]{1,0:T(8,128)} %get-tuple-element.42), channel_id=1, source_target_pairs={{0,9},{1,8},{2,11},{3,10},{4,12},{5,14},{6,13},{7,15},{8,1},{9,0},... | collective-permute-start | bytes 110600 | tf_op jit(solution)/shard_map/ppermute | solution.py:542
  10.0 4.5 %collective-permute-start.2 = (f32[8,128]{1,0:T(8,128)S(1)}, f32[8,128]{1,0:T(8,128)S(1)}, u32[]{:S(2)}, u32[]{:S(2)}) collective-permute-start(f32[8,128]{1,0:T(8,128)S(1)} %copy-done.3), channel_id=1, source_target_pairs={{0,24},{4,28},{8,16},{12,20},{16,8},{20,12},{24,0},{28,4},{1,25},{... | collective-permute-start | bytes 12296 | tf_op jit(solution)/shard_map/ppermute | solution.py:543
  10.5 1.2 %copy-start = (f32[16,32,512]{2,1,0:T(8,128)S(1)}, f32[16,32,512]{2,1,0:T(8,128)}, u32[]{:S(2)}) copy-start(f32[16,32,512]{2,1,0:T(8,128)} %sf_ref.3) | copy-start | bytes 3145732
  11.7 0.9 %copy-start.1 = (f32[32,16,64]{2,1,0:T(8,128)S(1)}, f32[32,16,64]{2,1,0:T(8,128)}, u32[]{:S(2)}) copy-start(f32[32,16,64]{2,1,0:T(8,128)} %sc_ref.1) | copy-start | bytes 393220
  14.5 1.6 %collective-permute-start.3 = (f32[32,128]{1,0:T(8,128)S(1)}, f32[32,128]{1,0:T(8,128)S(1)}, u32[]{:S(2)}, u32[]{:S(2)}) collective-permute-start(f32[32,128]{1,0:T(8,128)S(1)} %pad_maximum_fusion.par_ref.one_ref), channel_id=1, source_target_pairs={{0,4},{4,0},{8,12},{12,8},{16,20},{20,16},{24,28},{28,24},{1,5},{5... | collective-permute-start | bytes 49160 | tf_op jit(solution)/shard_map/ppermute | solution.py:548
  19.4 4.8 %collective-permute-start.4 = (f32[4,16,64]{2,1,0:T(8,128)S(1)}, f32[4,16,64]{2,1,0:T(8,128)S(1)}, u32[]{:S(2)}, u32[]{:S(2)}) collective-permute-start(f32[4,16,64]{2,1,0:T(8,128)S(1)} %fine_smooth.1), channel_id=1, source_target_pairs={{0,3},{1,14},{2,18},{3,31},{4,7},{5,10},{6,22},{7,27},{8,2},{9,15}... | collective-permute-start | bytes 49160 | tf_op jit(solution)/shard_map/ppermute | solution.py:574

commit v4 on v3

--- a/solution.py
+++ b/solution.py
@@ -186,11 +186,11 @@
     zt_ref[...] = jnp.where((row == terms) | (row == terms + 1), 1.0, zt)
 
 
-def members_of(pars, groups, nz, first_row, per_device, zt_ref, yz_ref):
+def members_of(pars, nz, first_row, per_device, zt_ref, yz_ref):
     weights = []
-    for par_ref in pars:
+    for par_ref, groups in pars:
         size = par_ref.shape[0]
-        for g in range(groups):
+        for g in groups:
             member = (LANES // nz) * g + iota((size, LANES), 1) // nz
             source = BLOCK * (member // per_device) + first_row + member % per_device
             pick = jnp.where(iota((size, LANES), 0) == source, 1.0, 0.0)
@@ -339,16 +339,12 @@
     return here.t * strip + here.half * nx, quarter(here.b, here.t, here.tiles) * ny
 
 
-def table_kernel(tiles, fine_sizes, coarse_sizes, mx_ref, my_ref, mz_ref, sf_ref, sc_ref, order_ref,
-                 fx_ref, fy_ref, fz_ref, ff_ref, cx_ref, cy_ref, cz_ref, cf_ref,
-                 tx_ref, ty_ref, own_ref, sem):
+def table_kernel(tiles, fine_sizes, coarse_sizes, mx_ref, my_ref, mz_ref, sf_ref, order_ref,
+                 fx_ref, fy_ref, fz_ref, ff_ref, cx_ref, cy_ref, cz_ref, tx_ref, ty_ref):
     here = Place(tiles)
     nx, ny, nz, full_x, full_y = fine_sizes
     strip = sf_ref.shape[0]
     count = nx + REACH
-    copy = pltpu.make_async_copy(
-        sf_ref.at[pl.ds(jnp.where(here.half == 0, 0, strip - count), count)], own_ref, sem)
-    copy.start()
     terms = mx_ref.shape[0]
     tx_ref[...] = jnp.zeros_like(tx_ref)
     tx_ref[0, 0:terms, 0:mx_ref.shape[1]] = mx_ref[...]
@@ -358,26 +354,16 @@
     x0, y0 = fine_place(here, strip, nx, ny)
     factors(1, terms, nx, ny, nz, x0, y0, full_x, full_y, tx_ref, ty_ref, fx_ref, fy_ref, fz_ref)
     shift = (EDGE + full_y - y0) % full_y
+    height = ff_ref.shape[1]
+    spread = spread_of(nz)
+    low = jnp.where(here.half == 0, 0, strip - count)
+    for k in range(count):
+        source = pltpu.roll(sf_ref[low + k], shift, 1)[:, :height]
+        ff_ref[k + REACH * (1 - here.half)] = force_of(source, spread)
 
     nx, ny, nz, full_x, full_y = coarse_sizes
-    x0 = here.m * nx
-    factors(2, terms, nx, ny, nz, x0, here.t * ny, full_x, full_y, tx_ref, ty_ref,
+    factors(2, terms, nx, ny, nz, here.m * nx, here.t * ny, full_x, full_y, tx_ref, ty_ref,
             cx_ref, cy_ref, cz_ref)
-    spread = spread_of(nz)
-    for k in range(nx + 2 * REACH):
-        x = jnp.clip(x0 - REACH + k, 0, full_x - 1)
-        cf_ref[k] = jnp.zeros_like(cf_ref[k])
-        cf_ref[k, EDGE:EDGE + ny, :] = force_of(sc_ref[x], spread)
-
-    copy.wait()
-    height = ff_ref.shape[1]
-    spread = spread_of(fine_sizes[2])
-
-    def place(k):
-        source = pltpu.roll(own_ref[k], shift, 1)[:, :height]
-        ff_ref[k + REACH * (1 - here.half)] = force_of(source, spread)
-
-    chunks(count, place)
 
 
 def fine_kernel(tiles, groups, sizes, strip, per_device,
@@ -387,7 +373,7 @@
     nx, ny, nz, full_x, full_y = sizes
     height = ny + 2 * EDGE
     x0, y0 = fine_place(here, strip, nx, ny)
-    weights = members_of((one_ref, two_ref), groups, nz, 0, per_device, z_ref, yz_ref)
+    weights = members_of(((one_ref, range(groups)), (two_ref, range(groups))), nz, 0, per_device, z_ref, yz_ref)
     spread = spread_of(nz)
     for k in range(REACH):
         edge_ref[k] = force_of(side_ref[k * nz:(k + 1) * nz, :height], spread)
@@ -407,32 +393,30 @@
            force, c_ref, kz_ref, q_ref, d_ref, e_ref, u_ref, finish)
 
 
-def coarse_kernel(tiles, groups, sizes, first_row, per_device,
-                  x_ref, y_ref, z_ref, f_ref, par_ref, base_ref, out_ref,
+def coarse_sweeps(here, sizes, weights, x_ref, y_ref, f_ref, base_ref, out_ref,
                   yz_ref, c_ref, kz_ref, q_ref, d_ref, e_ref, u_ref):
-    here = Place(tiles)
     nx, ny, nz, full_x, full_y = sizes
-    weights = members_of((par_ref,), groups, nz, first_row, per_device, z_ref, yz_ref)
-
-    def force(k, rows):
-        return f_ref[k, rows, :]
 
     def finish(j, value):
         out_ref[j] = value if base_ref is None else base_ref[j] + value
 
-    sweeps(groups, nx, ny, nz, here.m * nx, here.t * ny, full_x, full_y, False, weights, x_ref,
-           y_ref, yz_ref, force, c_ref, kz_ref, q_ref, d_ref, e_ref, u_ref, finish)
+    sweeps(len(weights), nx, ny, nz, here.m * nx, here.t * ny, full_x, full_y, False, weights,
+           x_ref, y_ref, yz_ref, lambda k, rows: f_ref[k, rows, :], c_ref, kz_ref, q_ref, d_ref,
+           e_ref, u_ref, finish)
 
 
 def coarse_near_kernel(tiles, groups, sizes, first_row, per_device, side_at,
-                       x_ref, y_ref, z_ref, f_ref, par_ref, a_ref, b_ref, out_ref, full_ref,
-                       *scratch_refs):
+                       x_ref, y_ref, z_ref, sc_ref, par_ref, a_ref, b_ref, out_ref, full_ref,
+                       yz_ref, *grids):
     here = Place(tiles)
-    nx, ny, nz, _, _ = sizes
+    nx, ny, nz, full_x, _ = sizes
     spread = spread_of(nz)
     per_group = side_at[2]
     for k in range(nx + 2 * REACH):
-        full_ref[k] = f_ref[k]
+        full_ref[k, 0:8, :] = jnp.zeros((8, LANES), jnp.float32)
+        full_ref[k, ny:ny + 2 * EDGE, :] = jnp.zeros((8, LANES), jnp.float32)
+        x = jnp.clip(here.m * nx - REACH + k, 0, full_x - 1)
+        full_ref[k, EDGE:EDGE + ny, :] = force_of(sc_ref[x], spread)
         rows = slice(k % per_group * nz, (k % per_group + 1) * nz)
         found = []
         for ref, at in ((a_ref, side_at[0]), (b_ref, side_at[1])):
@@ -443,8 +427,17 @@
         full_ref[k, EDGE - REACH:EDGE, :] = jnp.where(here.half == 0, found[0], found[1])
         full_ref[k, EDGE + ny:EDGE + ny + REACH, :] = jnp.where(
             here.half == 0, found[1], found[0])
-    coarse_kernel(tiles, groups, sizes, first_row, per_device, x_ref, y_ref, z_ref, full_ref,
-                  par_ref, None, out_ref, *scratch_refs)
+    weights = members_of(((par_ref, groups),), nz, first_row, per_device, z_ref, yz_ref)
+    coarse_sweeps(here, sizes, weights, x_ref, y_ref, full_ref, None, out_ref, yz_ref, *grids)
+
+
+def coarse_far_kernel(tiles, groups, twin_groups, sizes, first_row, per_device,
+                      x_ref, y_ref, z_ref, f_ref, par_ref, twin_ref, base_ref, out_ref,
+                      yz_ref, *grids):
+    here = Place(tiles)
+    weights = members_of(((par_ref, groups), (twin_ref, twin_groups)), sizes[2], first_row,
+                         per_device, z_ref, yz_ref)
+    coarse_sweeps(here, sizes, weights, x_ref, y_ref, f_ref, base_ref, out_ref, yz_ref, *grids)
 
 
 def scratch(groups, nx, ny, count):
@@ -527,16 +520,14 @@
 
         made = pl.pallas_call(
             functools.partial(table_kernel, tiles, fine_sizes, coarse_sizes),
-            out_shape=level_shapes(nx, ny) + level_shapes(cx, cy),
-            in_specs=[VMEM] * 3 + [HBM, VMEM, HBM],
-            out_specs=(VMEM,) * 8,
+            out_shape=level_shapes(nx, ny) + level_shapes(cx, cy)[:3],
+            in_specs=[VMEM] * 4 + [HBM],
+            out_specs=(VMEM,) * 7,
             scratch_shapes=[pltpu.VMEM((2, TERMS, LANES), jnp.float32),
-                            pltpu.VMEM((TERMS, full_y), jnp.float32),
-                            pltpu.VMEM((nx + REACH, nz, full_y), jnp.float32),
-                            pltpu.SemaphoreType.DMA],
+                            pltpu.VMEM((TERMS, full_y), jnp.float32)],
             compiler_params=limit(8),
             name="tables",
-        )(mode_x, mode_y, mode_z, source_fine, source_coarse, par)
+        )(mode_x, mode_y, mode_z, source_fine, par)
 
         side_a = lax.ppermute(side_a, axes, beside(bits[0], True))
         side_b = lax.ppermute(side_b, axes, beside(bits[1], False))
@@ -548,17 +539,18 @@
         twin = lax.ppermute(par, "member", [(i, i ^ 1) for i in range(members)])
 
         groups = tiles * n_coarse * cz // LANES
+        early = max(groups // 2, 1)
         part = jax.ShapeDtypeStruct((cx, cz, cy), jnp.float32)
         near, force = pl.pallas_call(
-            functools.partial(coarse_near_kernel, tiles, groups, coarse_sizes, n_fine, n_coarse,
-                              (height, EDGE * 2, rows // cz)),
+            functools.partial(coarse_near_kernel, tiles, range(early), coarse_sizes, n_fine,
+                              n_coarse, (height, EDGE * 2, rows // cz)),
             out_shape=(part, level_shapes(cx, cy)[3]),
             in_specs=[VMEM] * 7,
             out_specs=(VMEM, VMEM),
-            scratch_shapes=scratch(groups, cx, cy, cx),
+            scratch_shapes=scratch(early, cx, cy, cx),
             compiler_params=limit(16),
             name="coarse_near",
-        )(*of_coarse, par, side_a, side_b)
+        )(*of_coarse, source_coarse, par, side_a, side_b)
 
         fine_groups = tiles * n_fine * nz // LANES
         fine = pl.pallas_call(
@@ -574,14 +566,15 @@
         arrived = lax.ppermute(fine, axes, everywhere(owner))
 
         far = pl.pallas_call(
-            functools.partial(coarse_kernel, tiles, groups, coarse_sizes, n_fine, n_coarse),
+            functools.partial(coarse_far_kernel, tiles, range(early, groups), range(groups),
+                              coarse_sizes, n_fine, n_coarse),
             out_shape=part,
-            in_specs=[VMEM] * 6,
+            in_specs=[VMEM] * 7,
             out_specs=VMEM,
-            scratch_shapes=scratch(groups, cx, cy, cx),
+            scratch_shapes=scratch(2 * groups - early, cx, cy, cx),
             compiler_params=limit(16),
             name="coarse_far",
-        )(*of_coarse[:3], force, twin, near)
+        )(*of_coarse, force, par, twin, near)
         return arrived + far
 
     return jax.shard_map(

time: 25.1 us -> 24.7 us (0.984)
  waiting for transfers between devices: 2.29 us -> 3.45 us
  local copies, waits for them, and re-layouts: 2.19 us -> 1.25 us
  Pallas kernels: 10.6 us -> 9.96 us
    ppermute x1, waiting for transfers between devices: 0.31 us -> 1.88 us  [body(): lax.ppermute(par, 'member', [(i, i ^ 2 * d) for i in range(members)])]
    unnamed x12, local copies, waits for them, and re-layouts: 2.19 us -> 1.24 us
    pallas_call x1, Pallas kernels: 1.49 us -> 0.87 us  [body(): pl.pallas_call(functools.partial(table_kernel, tiles, fine_sizes, coarse_...]
    ppermute x1, waiting for transfers between devices: 1.97 us -> 1.56 us  [body(): arrived = lax.ppermute(fine, axes, everywhere(owner))]
  transfers between devices with their start and end apart: 5 -> 5, of which waited for: 2 -> 2; matrix products, arithmetic and copies ran while one was open for 0% -> 0% of each run, Pallas kernels for 18% -> 16%
where the time goes in v4:
time: 24.7 us; the launch traced here: 24.4 us
  Pallas kernels  9.96 us (40%)
  starting transfers between devices  8.42 us (34%)
  waiting for transfers between devices  3.45 us (14%)
  local copies, waits for them, and re-layouts  1.25 us (5%)
  between operations  0.74 us (3%)
  other arithmetic  0.62 us (3%)
    ppermute x1, starting transfers between devices, body(): side_b = lax.ppermute(side_b, axes, beside(bits[1], False))  3.52 us
    pallas_call x1, Pallas kernels, body(): pl.pallas_call(functools.partial(fine_kernel, tiles, fine_groups, fine_si...  3.28 us
    ppermute x1, starting transfers between devices, body(): side_a = lax.ppermute(side_a, axes, beside(bits[0], True))  3.06 us
    pallas_call x1, Pallas kernels, body(): pl.pallas_call(functools.partial(prep_kernel, tiles, nx, ny, cx, bits), o...  2.74 us
    pallas_call x1, Pallas kernels, body(): pl.pallas_call(functools.partial(coarse_far_kernel, tiles, range(early, g...  1.9 us
    ppermute x1, waiting for transfers between devices, body(): lax.ppermute(par, 'member', [(i, i ^ 2 * d) for i in range(members)])  1.88 us
    ppermute x1, waiting for transfers between devices, body(): arrived = lax.ppermute(fine, axes, everywhere(owner))  1.56 us
    ppermute x1, starting transfers between devices, body(): arrived = lax.ppermute(fine, axes, everywhere(owner))  1.37 us
  transfers between devices with their start and end apart: 5, of which 2 were waited for; matrix products, arithmetic and copies ran while one was open for 0% of the time, Pallas kernels for 16%

profile of v4, /device:TPU:0, one launch (start us, length us, event | category | flops | bytes accessed | tf_op | source)
XLA Modules:
  0.0 24.4 jit_solution(10652860243522044361)
XLA Ops:
  0.7 0.0 copy-start.2
  0.7 0.0 copy-start.4
  0.7 0.0 copy-start.5
  0.7 2.7 %prep.1 = (f32[72,256]{1,0:T(8,128)}, f32[72,128]{1,0:T(8,128)}, f32[8,128]{1,0:T(8,128)}) custom-call(s32[1,12]{1,0:T(1,128)} %nf_hbm.1, s32[4,12]{1,0:T(4,128)} %nc_hbm.1, s32[1]{0:T(128)S(6)} %copy.10.wf_ref, s32[4]{0:T(128)} %wc_ref.1, f32[16,32,512]{2,1,0:T(8,128)} %sf_ref.3, f32[32,16,64]{2,1,0:T(8,128)} %sc_ref.1), custom_call_target="tpu_custom_call" | custom-call | tf_op jit(solution)/shard_map/prep/pallas_call | solution.py:505
  3.4 0.0 copy-start.3
  3.4 3.1 %collective-permute-start = (f32[72,256]{1,0:T(8,128)}, f32[72,256]{1,0:T(8,128)S(1)}, u32[]{:S(2)}, u32[]{:S(2)}) collective-permute-start(f32[72,256]{1,0:T(8,128)} %get-tuple-element.38), channel_id=1, source_target_pairs={{0,16},{1,18},{2,17},{3,19},{4,21},{5,20},{6,23},{7,22},{8,24},{9,... | collective-permute-start | bytes 221192 | tf_op jit(solution)/shard_map/ppermute | solution.py:532
  6.5 3.5 %collective-permute-start.1 = (f32[72,128]{1,0:T(8,128)}, f32[72,128]{1,0:T(8,128)S(1)}, u32[]{:S(2)}, u32[]{:S(2)}) collective-permute-start(f32[72,128]{1,0:T(8,128)} %get-tuple-element.39), channel_id=1, source_target_pairs={{0,9},{1,8},{2,11},{3,10},{4,12},{5,14},{6,13},{7,15},{8,1},{9,0},... | collective-permute-start | bytes 110600 | tf_op jit(solution)/shard_map/ppermute | solution.py:533
  10.0 0.0 copy-done.3
  10.0 0.5 %collective-permute-start.2 = (f32[8,128]{1,0:T(8,128)S(1)}, f32[8,128]{1,0:T(8,128)S(1)}, u32[]{:S(2)}, u32[]{:S(2)}) collective-permute-start(f32[8,128]{1,0:T(8,128)S(1)} %copy-done.3), channel_id=1, source_target_pairs={{0,24},{4,28},{8,16},{12,20},{16,8},{20,12},{24,0},{28,4},{1,25},{... | collective-permute-start | bytes 12296 | tf_op jit(solution)/shard_map/ppermute | solution.py:534
  10.5 0.0 copy-done.2
  10.5 0.0 copy-done.4
  10.5 0.0 copy-done.5
  10.5 0.0 copy-start
  10.5 1.2 %copy-done = f32[16,32,512]{2,1,0:T(8,128)S(1)} copy-done((f32[16,32,512]{2,1,0:T(8,128)S(1)}, f32[16,32,512]{2,1,0:T(8,128)}, u32[]{:S(2)}) %copy-start) | copy-done | bytes 1048600
  11.7 0.0 copy-start.1
  11.7 0.9 %tables.1 = (f32[14,16,128]{2,1,0:T(8,128)S(1)}, bf16[136,96]{1,0:T(8,128)(2,1)S(1)}, f32[16,128]{1,0:T(8,128)S(1)}, f32[12,136,128]{2,1,0:T(8,128)S(1)}, f32[10...) custom-call(f32[12,64]{1,0:T(8,128)S(1)} %copy-done.4, f32[12,512]{1,0:T(8,128)S(1)} %copy-done.2, ...), custom_call_target="tpu_custom_call" | custom-call | tf_op jit(solution)/shard_map/tables/pallas_call | solution.py:521
  12.6 0.0 collective-permute-done.1.b_ref
  12.6 0.0 collective-permute-done.a_ref.side_ref
  12.6 1.9 %collective-permute-done.2 = f32[8,128]{1,0:T(8,128)S(1)} collective-permute-done((f32[8,128]{1,0:T(8,128)S(1)}, f32[8,128]{1,0:T(8,128)S(1)}, u32[]{:S(2)}, u32[]{:S(2)}) %collective-permute-start.2) | collective-permute-done | bytes 4128 | tf_op jit(solution)/shard_map/ppermute | solution.py:534
  14.5 0.0 collective-permute-start.3
  14.5 0.0 copy-done.1
  14.5 1.2 %coarse_near.1 = (f32[4,16,64]{2,1,0:T(8,128)S(1)}, f32[8,72,128]{2,1,0:T(8,128)S(1)}) custom-call(f32[10,16,128]{2,1,0:T(8,128)S(1)} %get-tuple-element.40.x_ref, bf16[72,96]{1,0:T(8,128)(2,1)S(1)} %get-tuple-element.41.y_ref, f32[16,128]{1,0:T(8,128)S(1)} %get-tuple-element.42.z_ref, f32[32,16,64]{2,1,0:T(8,128)S(1)} %copy-done.1, ...), custom_call_target="tpu_custom_call" | custom-call | tf_op jit(solution)/shard_map/coarse_near/pallas_call | solution.py:544
  15.7 0.0 collective-permute-done.3.two_ref.twin_ref
  15.7 3.3 %fine_smooth.1 = f32[4,16,64]{2,1,0:T(8,128)S(1)} custom-call(f32[14,16,128]{2,1,0:T(8,128)S(1)} %get-tuple-element.33.x_ref, bf16[136,96]{1,0:T(8,128)(2,1)S(1)} %get-tuple-element.34.y_ref, f32[16,128]{1,0:T(8,128)S(1)} %get-tuple-element.35.z_ref, f32[12,136,128]{2,1,0:T(8,128)S(1)} %get-tuple-element.36.f_ref, ...), custom_call_target="tpu_custom_call" | custom-call | tf_op jit(solution)/shard_map/fine_smooth/pallas_call | solution.py:556
  19.0 1.4 %collective-permute-start.4 = (f32[4,16,64]{2,1,0:T(8,128)S(1)}, f32[4,16,64]{2,1,0:T(8,128)S(1)}, u32[]{:S(2)}, u32[]{:S(2)}) collective-permute-start(f32[4,16,64]{2,1,0:T(8,128)S(1)} %fine_smooth.1), channel_id=1, source_target_pairs={{0,3},{1,14},{2,18},{3,31},{4,7},{5,10},{6,22},{7,27},{8,2},{9,15}... | collective-permute-start | bytes 49160 | tf_op jit(solution)/shard_map/ppermute | solution.py:566
  20.4 1.9 %coarse_far.1 = f32[4,16,64]{2,1,0:T(8,128)S(1)} custom-call(f32[10,16,128]{2,1,0:T(8,128)S(1)} %get-tuple-element.40.x_ref, bf16[72,96]{1,0:T(8,128)(2,1)S(1)} %get-tuple-element.41.y_ref, f32[16,128]{1,0:T(8,128)S(1)} %get-tuple-element.42.z_ref, f32[8,72,128]{2,1,0:T(8,128)S(1)} %get-tuple-element.44.f_ref, ...), custom_call_target="tpu_custom_call" | custom-call | tf_op jit(solution)/shard_map/coarse_far/pallas_call | solution.py:568
  22.3 1.6 %collective-permute-done.4 = f32[4,16,64]{2,1,0:T(8,128)S(1)} collective-permute-done((f32[4,16,64]{2,1,0:T(8,128)S(1)}, f32[4,16,64]{2,1,0:T(8,128)S(1)}, u32[]{:S(2)}, u32[]{:S(2)}) %collective-permute-start.4) | collective-permute-done | bytes 16416 | tf_op jit(solution)/shard_map/ppermute | solution.py:566
  23.8 0.6 %add.3 = f32[4,16,64]{2,1,0:T(8,128)} add(f32[4,16,64]{2,1,0:T(8,128)S(1)} %collective-permute-done.4, f32[4,16,64]{2,1,0:T(8,128)S(1)} %coarse_far.1) | non-fusion elementwise | flops 4096 | bytes 49152 | tf_op jit(solution)/shard_map/add | solution.py:578
  (3 shorter events, 0.0 us)
Async XLA Ops:
  0.7 9.8 %copy-start.2 = (f32[12,512]{1,0:T(8,128)S(1)}, f32[12,512]{1,0:T(8,128)}, u32[]{:S(2)}) copy-start(f32[12,512]{1,0:T(8,128)} %my_ref.1) | copy-start | bytes 73732
  0.7 9.8 %copy-start.4 = (f32[12,64]{1,0:T(8,128)S(1)}, f32[12,64]{1,0:T(8,128)}, u32[]{:S(2)}) copy-start(f32[12,64]{1,0:T(8,128)} %mx_ref.1) | copy-start | bytes 9220
  0.7 9.8 %copy-start.5 = (f32[12,32]{1,0:T(8,128)S(1)}, f32[12,32]{1,0:T(8,128)}, u32[]{:S(2)}) copy-start(f32[12,32]{1,0:T(8,128)} %mz_ref.1) | copy-start | bytes 4612
  3.4 6.6 %copy-start.3 = (f32[8,128]{1,0:T(8,128)S(1)}, f32[8,128]{1,0:T(8,128)}, u32[]{:S(2)}) copy-start(f32[8,128]{1,0:T(8,128)} %get-tuple-element.37.order_ref) | copy-start | bytes 12292
  3.4 9.2 %collective-permute-start = (f32[72,256]{1,0:T(8,128)}, f32[72,256]{1,0:T(8,128)S(1)}, u32[]{:S(2)}, u32[]{:S(2)}) collective-permute-start(f32[72,256]{1,0:T(8,128)} %get-tuple-element.38), channel_id=1, source_target_pairs={{0,16},{1,18},{2,17},{3,19},{4,21},{5,20},{6,23},{7,22},{8,24},{9,... | collective-permute-start | bytes 221192 | tf_op jit(solution)/shard_map/ppermute | solution.py:532
  6.5 6.1 %collective-permute-start.1 = (f32[72,128]{1,0:T(8,128)}, f32[72,128]{1,0:T(8,128)S(1)}, u32[]{:S(2)}, u32[]{:S(2)}) collective-permute-start(f32[72,128]{1,0:T(8,128)} %get-tuple-element.39), channel_id=1, source_target_pairs={{0,9},{1,8},{2,11},{3,10},{4,12},{5,14},{6,13},{7,15},{8,1},{9,0},... | collective-permute-start | bytes 110600 | tf_op jit(solution)/shard_map/ppermute | solution.py:533
  10.0 4.5 %collective-permute-start.2 = (f32[8,128]{1,0:T(8,128)S(1)}, f32[8,128]{1,0:T(8,128)S(1)}, u32[]{:S(2)}, u32[]{:S(2)}) collective-permute-start(f32[8,128]{1,0:T(8,128)S(1)} %copy-done.3), channel_id=1, source_target_pairs={{0,24},{4,28},{8,16},{12,20},{16,8},{20,12},{24,0},{28,4},{1,25},{... | collective-permute-start | bytes 12296 | tf_op jit(solution)/shard_map/ppermute | solution.py:534
  10.5 1.2 %copy-start = (f32[16,32,512]{2,1,0:T(8,128)S(1)}, f32[16,32,512]{2,1,0:T(8,128)}, u32[]{:S(2)}) copy-start(f32[16,32,512]{2,1,0:T(8,128)} %sf_ref.3) | copy-start | bytes 3145732
  11.7 2.8 %copy-start.1 = (f32[32,16,64]{2,1,0:T(8,128)S(1)}, f32[32,16,64]{2,1,0:T(8,128)}, u32[]{:S(2)}) copy-start(f32[32,16,64]{2,1,0:T(8,128)} %sc_ref.1) | copy-start | bytes 393220
  14.5 1.2 %collective-permute-start.3 = (f32[32,128]{1,0:T(8,128)S(1)}, f32[32,128]{1,0:T(8,128)S(1)}, u32[]{:S(2)}, u32[]{:S(2)}) collective-permute-start(f32[32,128]{1,0:T(8,128)S(1)} %pad_maximum_fusion.par_ref.one_ref), channel_id=1, source_target_pairs={{0,4},{4,0},{8,12},{12,8},{16,20},{20,16},{24,28},{28,24},{1,5},{5... | collective-permute-start | bytes 49160 | tf_op jit(solution)/shard_map/ppermute | solution.py:539
  19.0 4.8 %collective-permute-start.4 = (f32[4,16,64]{2,1,0:T(8,128)S(1)}, f32[4,16,64]{2,1,0:T(8,128)S(1)}, u32[]{:S(2)}, u32[]{:S(2)}) collective-permute-start(f32[4,16,64]{2,1,0:T(8,128)S(1)} %fine_smooth.1), channel_id=1, source_target_pairs={{0,3},{1,14},{2,18},{3,31},{4,7},{5,10},{6,22},{7,27},{8,2},{9,15}... | collective-permute-start | bytes 49160 | tf_op jit(solution)/shard_map/ppermute | solution.py:566

commit v5 on v4

--- a/solution.py
+++ b/solution.py
@@ -79,8 +79,8 @@
         return jnp.where((to >= 0) & (to < self.tiles), to, self.t)
 
 
-def prep_kernel(tiles, nx, ny, cx, bits, nf_hbm, nc_hbm, wf_ref, wc_ref, sf_ref, sc_hbm,
-                a_ref, b_ref, par_ref, plane_ref, nf_ref, nc_ref, sc_ref, sems):
+def prep_kernel(tiles, nx, ny, cx, bits, terms, count, pk_ref, sf_ref, sc_hbm,
+                a_ref, b_ref, par_ref, plane_ref, sc_ref, sems):
     here = Place(tiles)
     strip, nz, full_y = sf_ref.shape
     full_x, cz, cy = sc_hbm.shape
@@ -90,32 +90,21 @@
     copy.start()
     window = cx + 2 * REACH
     lows = [jnp.clip(cx * ((here.b ^ bit) * 2 + here.a) - REACH, 0, full_x - window) for bit in bits]
-    blocks = [pltpu.make_async_copy(sc_hbm.at[pl.ds(lows[k], window)], sc_ref.at[k], sems.at[3 + k])
+    blocks = [pltpu.make_async_copy(sc_hbm.at[pl.ds(lows[k], window)], sc_ref.at[k], sems.at[1 + k])
               for k in range(2)]
-    nodes = [pltpu.make_async_copy(nf_hbm, nf_ref, sems.at[1]),
-             pltpu.make_async_copy(nc_hbm, nc_ref, sems.at[2])]
-    for item in nodes + blocks:
+    for item in blocks:
         item.start()
-    for item in nodes:
-        item.wait()
-
-    def node_values(ref):
-        nodes = ref[...]
-        out = jnp.zeros(nodes.shape, jnp.float32)
-        for k in range(NODES):
-            out = jnp.where(nodes == k, math.cos(math.pi * k / (NODES - 1)), out)
-        return out
-
-    n_fine, terms = nf_ref.shape
-    n_coarse = nc_ref.shape[0]
-    row, lane = iota((BLOCK, LANES), 0), iota((BLOCK, LANES), 1)
-    base = jnp.where((lane == terms) | (lane == terms + 1), 1.0, 0.0)
-    for k in range(n_fine + n_coarse):
-        weight = wf_ref[k] if k < n_fine else wc_ref[k - n_fine]
-        base = jnp.where((row == k) & (lane == terms + 2), weight.astype(jnp.float32), base)
-    par_ref[...] = base
-    par_ref[0:n_fine, 0:terms] = node_values(nf_ref)
-    par_ref[n_fine:n_fine + n_coarse, 0:terms] = node_values(nc_ref)
+
+    packed = pk_ref[...]
+    lane = iota(packed.shape, 1)
+    row = iota(packed.shape, 0)
+    weight = jnp.broadcast_to(packed[count:count + 1, :].astype(jnp.float32), packed.shape)
+    weight = jnp.sum(jnp.where(lane == row, weight, 0.0), axis=1, keepdims=True)
+    out = jnp.where((lane == terms) | (lane == terms + 1), 1.0, 0.0)
+    out = jnp.where((lane == terms + 2) & (row < count), weight, out)
+    for k in range(NODES):
+        out = jnp.where((lane < terms) & (packed == k), math.cos(math.pi * k / (NODES - 1)), out)
+    par_ref[...] = out
 
     rows = REACH * nz
     per_group = rows // cz
@@ -502,21 +491,26 @@
         fine_sizes = nx, ny, nz, full_x, full_y
         coarse_sizes = cx, cy, cz, full_cx, cy * tiles
 
+        terms, count = mode_x.shape[0], n_fine + n_coarse
+        packed = (
+            jnp.pad(node_fine, ((0, BLOCK - n_fine), (0, LANES - terms)))
+            + jnp.pad(node_coarse, ((n_fine, BLOCK - count), (0, LANES - terms)))
+            + jnp.pad(weight_fine[None, :], ((count, BLOCK - count - 1), (0, LANES - n_fine)))
+            + jnp.pad(weight_coarse[None, :],
+                      ((count, BLOCK - count - 1), (n_fine, LANES - count))))
         side_a, side_b, par = pl.pallas_call(
-            functools.partial(prep_kernel, tiles, nx, ny, cx, bits),
+            functools.partial(prep_kernel, tiles, nx, ny, cx, bits, terms, count),
             out_shape=(jax.ShapeDtypeStruct((rows + BLOCK, width), jnp.float32),
                        jax.ShapeDtypeStruct((rows + BLOCK, LANES), jnp.float32),
                        jax.ShapeDtypeStruct((BLOCK, LANES), jnp.float32)),
-            in_specs=[FIXED, FIXED, SMEM, SMEM, FIXED, FIXED],
+            in_specs=[VMEM, HBM, HBM],
             out_specs=(VMEM, VMEM, VMEM),
             scratch_shapes=[pltpu.VMEM((REACH, nz, full_y), jnp.float32),
-                            pltpu.VMEM(node_fine.shape, jnp.int32),
-                            pltpu.VMEM(node_coarse.shape, jnp.int32),
                             pltpu.VMEM((2, cx + 2 * REACH, cz, cy), jnp.float32),
-                            pltpu.SemaphoreType.DMA((5,))],
-            compiler_params=pltpu.CompilerParams(vmem_limit_bytes=67043328 - (200 << 10)),
+                            pltpu.SemaphoreType.DMA((3,))],
+            compiler_params=pltpu.CompilerParams(vmem_limit_bytes=67043328 - (10480 << 10)),
             name="prep",
-        )(node_fine, node_coarse, weight_fine, weight_coarse, source_fine, source_coarse)
+        )(packed, source_fine, source_coarse)
 
         made = pl.pallas_call(
             functools.partial(table_kernel, tiles, fine_sizes, coarse_sizes),

time: 24.7 us -> 24 us (0.972)
  Pallas kernels: 9.96 us -> 8.51 us
  waiting for transfers between devices: 3.45 us -> 4.7 us
  local copies, waits for them, and re-layouts: 1.25 us -> 0.02 us
  other arithmetic: 0.62 us -> 1.39 us
    pallas_call x1, Pallas kernels: 2.74 us -> 1.29 us  [body(): pl.pallas_call(functools.partial(prep_kernel, tiles, nx, ny, cx, bits, te...]
    unnamed x12 -> x10, local copies, waits for them, and re-layouts: 1.24 us -> 0.02 us
    add x0 -> x1, other arithmetic: none -> 0.77 us  [body(): jnp.pad(node_fine, ((0, BLOCK - n_fine), (0, LANES - terms)))]
    ppermute x1, waiting for transfers between devices: 1.88 us -> 2.57 us  [body(): lax.ppermute(par, 'member', [(i, i ^ 2 * d) for i in range(members)])]
    ppermute x1, waiting for transfers between devices: 0.01 us -> 0.56 us  [body(): side_b = lax.ppermute(side_b, axes, beside(bits[1], False))]
  transfers between devices with their start and end apart: 5 -> 5, of which waited for: 2 -> 3; matrix products, arithmetic and copies ran while one was open for 0% -> 0% of each run, Pallas kernels for 16% -> 17%
where the time goes in v5:
time: 24 us; the launch traced here: 23.8 us
  Pallas kernels  8.51 us (35%)
  starting transfers between devices  8.42 us (35%)
  waiting for transfers between devices  4.7 us (20%)
  other arithmetic  1.39 us (6%)
  between operations  0.77 us (3%)
    ppermute x1, starting transfers between devices, body(): side_b = lax.ppermute(side_b, axes, beside(bits[1], False))  3.52 us
    pallas_call x1, Pallas kernels, body(): pl.pallas_call(functools.partial(fine_kernel, tiles, fine_groups, fine_si...  3.27 us
    ppermute x1, starting transfers between devices, body(): side_a = lax.ppermute(side_a, axes, beside(bits[0], True))  3.06 us
    ppermute x1, waiting for transfers between devices, body(): lax.ppermute(par, 'member', [(i, i ^ 2 * d) for i in range(members)])  2.57 us
    pallas_call x1, Pallas kernels, body(): pl.pallas_call(functools.partial(coarse_far_kernel, tiles, range(early, g...  1.9 us
    ppermute x1, waiting for transfers between devices, body(): arrived = lax.ppermute(fine, axes, everywhere(owner))  1.56 us
    ppermute x1, starting transfers between devices, body(): arrived = lax.ppermute(fine, axes, everywhere(owner))  1.37 us
    pallas_call x1, Pallas kernels, body(): pl.pallas_call(functools.partial(prep_kernel, tiles, nx, ny, cx, bits, te...  1.29 us
  transfers between devices with their start and end apart: 5, of which 3 were waited for; matrix products, arithmetic and copies ran while one was open for 0% of the time, Pallas kernels for 17%

profile of v5, /device:TPU:0, one launch (start us, length us, event | category | flops | bytes accessed | tf_op | source)
XLA Modules:
  0.0 23.8 jit_solution(7734656562766144895)
XLA Ops:
  0.0 0.0 copy-start
  0.7 0.8 %pad_add_fusion.pk_ref = s32[8,128]{1,0:T(8,128)S(1)} fusion(s32[1,4]{1,0:T(1,128)} %bitcast.3, s32[1,1]{1,0:T(1,128)} %bitcast.2, s32[4,12]{1,0:T(4,128)} %param.10, s32[1,12]{1,0:T(1,128)} %param.9), kind=kLoop, calls=%fused_computation.1 | loop fusion | flops 3072 | bytes 4356 | tf_op jit(solution)/shard_map/add | solution.py:496
  1.5 0.0 copy-start.2
  1.5 0.0 copy-start.3
  1.5 0.0 copy-start.4
  1.5 1.3 %prep.1 = (f32[72,256]{1,0:T(8,128)S(1)}, f32[72,128]{1,0:T(8,128)S(1)}, f32[8,128]{1,0:T(8,128)S(1)}) custom-call(s32[8,128]{1,0:T(8,128)S(1)} %pad_add_fusion.pk_ref, f32[16,32,512]{2,1,0:T(8,128)} %sf_ref.3, f32[32,16,64]{2,1,0:T(8,128)} %sc_ref.1), custom_call_target="tpu_custom_call" | custom-call | tf_op jit(solution)/shard_map/prep/pallas_call | solution.py:501
  2.8 3.1 %collective-permute-start = (f32[72,256]{1,0:T(8,128)S(1)}, f32[72,256]{1,0:T(8,128)S(1)}, u32[]{:S(2)}, u32[]{:S(2)}) collective-permute-start(f32[72,256]{1,0:T(8,128)S(1)} %get-tuple-element.38), channel_id=1, source_target_pairs={{0,16},{1,18},{2,17},{3,19},{4,21},{5,20},{6,23},{7,22},{8,24},{9,... | collective-permute-start | bytes 221192 | tf_op jit(solution)/shard_map/ppermute | solution.py:526
  5.9 3.5 %collective-permute-start.1 = (f32[72,128]{1,0:T(8,128)S(1)}, f32[72,128]{1,0:T(8,128)S(1)}, u32[]{:S(2)}, u32[]{:S(2)}) collective-permute-start(f32[72,128]{1,0:T(8,128)S(1)} %get-tuple-element.39), channel_id=1, source_target_pairs={{0,9},{1,8},{2,11},{3,10},{4,12},{5,14},{6,13},{7,15},{8,1},{9,0},... | collective-permute-start | bytes 110600 | tf_op jit(solution)/shard_map/ppermute | solution.py:527
  9.4 0.0 copy-start.1
  9.4 0.5 %collective-permute-start.2 = (f32[8,128]{1,0:T(8,128)S(1)}, f32[8,128]{1,0:T(8,128)S(1)}, u32[]{:S(2)}, u32[]{:S(2)}) collective-permute-start(f32[8,128]{1,0:T(8,128)S(1)} %get-tuple-element.37.order_ref), channel_id=1, source_target_pairs={{0,24},{4,28},{8,16},{12,20},{16,8},{20,12},{24,0},{28,4},{1,25},{... | collective-permute-start | bytes 12296 | tf_op jit(solution)/shard_map/ppermute | solution.py:528
  9.9 0.0 copy-done
  9.9 0.0 copy-done.2
  9.9 0.0 copy-done.3
  9.9 0.0 copy-done.4
  9.9 0.9 %tables.1 = (f32[14,16,128]{2,1,0:T(8,128)S(1)}, bf16[136,96]{1,0:T(8,128)(2,1)S(1)}, f32[16,128]{1,0:T(8,128)S(1)}, f32[12,136,128]{2,1,0:T(8,128)S(1)}, f32[10...) custom-call(f32[12,64]{1,0:T(8,128)S(1)} %copy-done.3, f32[12,512]{1,0:T(8,128)S(1)} %copy-done.2, ...), custom_call_target="tpu_custom_call" | custom-call | tf_op jit(solution)/shard_map/tables/pallas_call | solution.py:515
  10.8 0.6 %collective-permute-done.1.b_ref = f32[72,128]{1,0:T(8,128)S(1)} collective-permute-done((f32[72,128]{1,0:T(8,128)S(1)}, f32[72,128]{1,0:T(8,128)S(1)}, u32[]{:S(2)}, u32[]{:S(2)}) %collective-permute-start.1) | collective-permute-done | bytes 36896 | tf_op jit(solution)/shard_map/ppermute | solution.py:527
  11.3 0.0 collective-permute-done.a_ref.side_ref
  11.3 2.6 %collective-permute-done.2 = f32[8,128]{1,0:T(8,128)S(1)} collective-permute-done((f32[8,128]{1,0:T(8,128)S(1)}, f32[8,128]{1,0:T(8,128)S(1)}, u32[]{:S(2)}, u32[]{:S(2)}) %collective-permute-start.2) | collective-permute-done | bytes 4128 | tf_op jit(solution)/shard_map/ppermute | solution.py:528
  13.9 0.0 collective-permute-start.3
  13.9 0.0 copy-done.1
  13.9 1.2 %coarse_near.1 = (f32[4,16,64]{2,1,0:T(8,128)S(1)}, f32[8,72,128]{2,1,0:T(8,128)S(1)}) custom-call(f32[10,16,128]{2,1,0:T(8,128)S(1)} %get-tuple-element.40.x_ref, bf16[72,96]{1,0:T(8,128)(2,1)S(1)} %get-tuple-element.41.y_ref, f32[16,128]{1,0:T(8,128)S(1)} %get-tuple-element.42.z_ref, f32[32,16,64]{2,1,0:T(8,128)S(1)} %copy-done.1, ...), custom_call_target="tpu_custom_call" | custom-call | tf_op jit(solution)/shard_map/coarse_near/pallas_call | solution.py:538
  15.1 0.0 collective-permute-done.3.two_ref.twin_ref
  15.1 3.3 %fine_smooth.1 = f32[4,16,64]{2,1,0:T(8,128)S(1)} custom-call(f32[14,16,128]{2,1,0:T(8,128)S(1)} %get-tuple-element.33.x_ref, bf16[136,96]{1,0:T(8,128)(2,1)S(1)} %get-tuple-element.34.y_ref, f32[16,128]{1,0:T(8,128)S(1)} %get-tuple-element.35.z_ref, f32[12,136,128]{2,1,0:T(8,128)S(1)} %get-tuple-element.36.f_ref, ...), custom_call_target="tpu_custom_call" | custom-call | tf_op jit(solution)/shard_map/fine_smooth/pallas_call | solution.py:550
  18.4 1.4 %collective-permute-start.4 = (f32[4,16,64]{2,1,0:T(8,128)S(1)}, f32[4,16,64]{2,1,0:T(8,128)S(1)}, u32[]{:S(2)}, u32[]{:S(2)}) collective-permute-start(f32[4,16,64]{2,1,0:T(8,128)S(1)} %fine_smooth.1), channel_id=1, source_target_pairs={{0,3},{1,14},{2,18},{3,31},{4,7},{5,10},{6,22},{7,27},{8,2},{9,15}... | collective-permute-start | bytes 49160 | tf_op jit(solution)/shard_map/ppermute | solution.py:560
  19.7 1.9 %coarse_far.1 = f32[4,16,64]{2,1,0:T(8,128)S(1)} custom-call(f32[10,16,128]{2,1,0:T(8,128)S(1)} %get-tuple-element.40.x_ref, bf16[72,96]{1,0:T(8,128)(2,1)S(1)} %get-tuple-element.41.y_ref, f32[16,128]{1,0:T(8,128)S(1)} %get-tuple-element.42.z_ref, f32[8,72,128]{2,1,0:T(8,128)S(1)} %get-tuple-element.44.f_ref, ...), custom_call_target="tpu_custom_call" | custom-call | tf_op jit(solution)/shard_map/coarse_far/pallas_call | solution.py:562
  21.6 1.6 %collective-permute-done.4 = f32[4,16,64]{2,1,0:T(8,128)S(1)} collective-permute-done((f32[4,16,64]{2,1,0:T(8,128)S(1)}, f32[4,16,64]{2,1,0:T(8,128)S(1)}, u32[]{:S(2)}, u32[]{:S(2)}) %collective-permute-start.4) | collective-permute-done | bytes 16416 | tf_op jit(solution)/shard_map/ppermute | solution.py:560
  23.2 0.6 %add.23 = f32[4,16,64]{2,1,0:T(8,128)} add(f32[4,16,64]{2,1,0:T(8,128)S(1)} %collective-permute-done.4, f32[4,16,64]{2,1,0:T(8,128)S(1)} %coarse_far.1) | non-fusion elementwise | flops 4096 | bytes 49152 | tf_op jit(solution)/shard_map/add | solution.py:572
  (3 shorter events, 0.0 us)
Async XLA Ops:
  0.0 9.9 %copy-start = (f32[16,32,512]{2,1,0:T(8,128)S(1)}, f32[16,32,512]{2,1,0:T(8,128)}, u32[]{:S(2)}) copy-start(f32[16,32,512]{2,1,0:T(8,128)} %sf_ref.3) | copy-start | bytes 3145732
  1.5 8.4 %copy-start.2 = (f32[12,512]{1,0:T(8,128)S(1)}, f32[12,512]{1,0:T(8,128)}, u32[]{:S(2)}) copy-start(f32[12,512]{1,0:T(8,128)} %my_ref.1) | copy-start | bytes 73732
  1.5 8.4 %copy-start.3 = (f32[12,64]{1,0:T(8,128)S(1)}, f32[12,64]{1,0:T(8,128)}, u32[]{:S(2)}) copy-start(f32[12,64]{1,0:T(8,128)} %mx_ref.1) | copy-start | bytes 9220
  1.5 8.4 %copy-start.4 = (f32[12,32]{1,0:T(8,128)S(1)}, f32[12,32]{1,0:T(8,128)}, u32[]{:S(2)}) copy-start(f32[12,32]{1,0:T(8,128)} %mz_ref.1) | copy-start | bytes 4612
  2.8 8.5 %collective-permute-start = (f32[72,256]{1,0:T(8,128)S(1)}, f32[72,256]{1,0:T(8,128)S(1)}, u32[]{:S(2)}, u32[]{:S(2)}) collective-permute-start(f32[72,256]{1,0:T(8,128)S(1)} %get-tuple-element.38), channel_id=1, source_target_pairs={{0,16},{1,18},{2,17},{3,19},{4,21},{5,20},{6,23},{7,22},{8,24},{9,... | collective-permute-start | bytes 221192 | tf_op jit(solution)/shard_map/ppermute | solution.py:526
  5.9 5.5 %collective-permute-start.1 = (f32[72,128]{1,0:T(8,128)S(1)}, f32[72,128]{1,0:T(8,128)S(1)}, u32[]{:S(2)}, u32[]{:S(2)}) collective-permute-start(f32[72,128]{1,0:T(8,128)S(1)} %get-tuple-element.39), channel_id=1, source_target_pairs={{0,9},{1,8},{2,11},{3,10},{4,12},{5,14},{6,13},{7,15},{8,1},{9,0},... | collective-permute-start | bytes 110600 | tf_op jit(solution)/shard_map/ppermute | solution.py:527
  9.4 4.5 %copy-start.1 = (f32[32,16,64]{2,1,0:T(8,128)S(1)}, f32[32,16,64]{2,1,0:T(8,128)}, u32[]{:S(2)}) copy-start(f32[32,16,64]{2,1,0:T(8,128)} %sc_ref.1) | copy-start | bytes 393220
  9.4 4.5 %collective-permute-start.2 = (f32[8,128]{1,0:T(8,128)S(1)}, f32[8,128]{1,0:T(8,128)S(1)}, u32[]{:S(2)}, u32[]{:S(2)}) collective-permute-start(f32[8,128]{1,0:T(8,128)S(1)} %get-tuple-element.37.order_ref), channel_id=1, source_target_pairs={{0,24},{4,28},{8,16},{12,20},{16,8},{20,12},{24,0},{28,4},{1,25},{... | collective-permute-start | bytes 12296 | tf_op jit(solution)/shard_map/ppermute | solution.py:528
  13.9 1.2 %collective-permute-start.3 = (f32[32,128]{1,0:T(8,128)S(1)}, f32[32,128]{1,0:T(8,128)S(1)}, u32[]{:S(2)}, u32[]{:S(2)}) collective-permute-start(f32[32,128]{1,0:T(8,128)S(1)} %pad_maximum_fusion.par_ref.one_ref), channel_id=1, source_target_pairs={{0,4},{4,0},{8,12},{12,8},{16,20},{20,16},{24,28},{28,24},{1,5},{5... | collective-permute-start | bytes 49160 | tf_op jit(solution)/shard_map/ppermute | solution.py:533
  18.4 4.8 %collective-permute-start.4 = (f32[4,16,64]{2,1,0:T(8,128)S(1)}, f32[4,16,64]{2,1,0:T(8,128)S(1)}, u32[]{:S(2)}, u32[]{:S(2)}) collective-permute-start(f32[4,16,64]{2,1,0:T(8,128)S(1)} %fine_smooth.1), channel_id=1, source_target_pairs={{0,3},{1,14},{2,18},{3,31},{4,7},{5,10},{6,22},{7,27},{8,2},{9,15}... | collective-permute-start | bytes 49160 | tf_op jit(solution)/shard_map/ppermute | solution.py:560

commit v6 on v5

--- a/solution.py
+++ b/solution.py
@@ -7,6 +7,7 @@
 from jax.experimental import pallas as pl
 from jax.experimental.pallas import tpu as pltpu
 from jax.sharding import PartitionSpec as P
+
 
 NODES = 9
 SWEEPS = 3
@@ -79,7 +80,7 @@
         return jnp.where((to >= 0) & (to < self.tiles), to, self.t)
 
 
-def prep_kernel(tiles, nx, ny, cx, bits, terms, count, pk_ref, sf_ref, sc_hbm,
+def prep_kernel(tiles, ny, cx, bits, terms, count, pk_ref, sf_ref, sc_hbm,
                 a_ref, b_ref, par_ref, plane_ref, sc_ref, sems):
     here = Place(tiles)
     strip, nz, full_y = sf_ref.shape
@@ -473,6 +474,7 @@
             step = 1 if a ^ (t % 2) else -1
             to = t + (step if outward else -step)
             return b ^ bit, a, to if 0 <= to < tiles else t
+
         return everywhere(rule)
 
     def owner(b, a, t):
@@ -499,7 +501,7 @@
             + jnp.pad(weight_coarse[None, :],
                       ((count, BLOCK - count - 1), (n_fine, LANES - count))))
         side_a, side_b, par = pl.pallas_call(
-            functools.partial(prep_kernel, tiles, nx, ny, cx, bits, terms, count),
+            functools.partial(prep_kernel, tiles, ny, cx, bits, terms, count),
             out_shape=(jax.ShapeDtypeStruct((rows + BLOCK, width), jnp.float32),
                        jax.ShapeDtypeStruct((rows + BLOCK, LANES), jnp.float32),
                        jax.ShapeDtypeStruct((BLOCK, LANES), jnp.float32)),
@@ -525,8 +527,9 @@
 
         side_a = lax.ppermute(side_a, axes, beside(bits[0], True))
         side_b = lax.ppermute(side_b, axes, beside(bits[1], False))
-        more = [lax.ppermute(par, "member", [(i, i ^ (2 * d)) for i in range(members)])
-                for d in others]
+        more = []
+        for d in others:
+            more.append(lax.ppermute(par, "member", [(i, i ^ (2 * d)) for i in range(members)]))
         par, made = lax.optimization_barrier((par, made))
         of_fine, of_coarse = made[:4], made[4:]
         par = jnp.concatenate([par, side_a[rows:, :LANES], side_b[rows:]] + more, axis=0)

time: 24 us -> 24 us (level)
  no operation moved by 1% of the time
where the time goes in v6:
time: 24 us; the launch traced here: 23.8 us
  Pallas kernels  8.51 us (35%)
  starting transfers between devices  8.42 us (35%)
  waiting for transfers between devices  4.7 us (20%)
  other arithmetic  1.39 us (6%)
  between operations  0.77 us (3%)
    ppermute x1, starting transfers between devices, body(): side_b = lax.ppermute(side_b, axes, beside(bits[1], False))  3.52 us
    pallas_call x1, Pallas kernels, body(): pl.pallas_call(functools.partial(fine_kernel, tiles, fine_groups, fine_si...  3.27 us
    ppermute x1, starting transfers between devices, body(): side_a = lax.ppermute(side_a, axes, beside(bits[0], True))  3.06 us
    ppermute x1, waiting for transfers between devices, body(): lax.ppermute(par, 'member', [(i, i ^ 2 * d) for i in range(members)])  2.57 us
    pallas_call x1, Pallas kernels, body(): pl.pallas_call(functools.partial(coarse_far_kernel, tiles, range(early, g...  1.9 us
    ppermute x1, waiting for transfers between devices, body(): arrived = lax.ppermute(fine, axes, everywhere(owner))  1.56 us
    ppermute x1, starting transfers between devices, body(): arrived = lax.ppermute(fine, axes, everywhere(owner))  1.37 us
    pallas_call x1, Pallas kernels, body(): pl.pallas_call(functools.partial(prep_kernel, tiles, ny, cx, bits, terms,...  1.29 us
  transfers between devices with their start and end apart: 5, of which 3 were waited for; matrix products, arithmetic and copies ran while one was open for 0% of the time, Pallas kernels for 17%

profile of v6, /device:TPU:0, one launch (start us, length us, event | category | flops | bytes accessed | tf_op | source)
XLA Modules:
  0.0 23.8 jit_solution(7734656562766144895)
XLA Ops:
  0.0 0.0 copy-start
  0.7 0.8 %pad_add_fusion.pk_ref = s32[8,128]{1,0:T(8,128)S(1)} fusion(s32[1,4]{1,0:T(1,128)} %bitcast.3, s32[1,1]{1,0:T(1,128)} %bitcast.2, s32[4,12]{1,0:T(4,128)} %param.10, s32[1,12]{1,0:T(1,128)} %param.9), kind=kLoop, calls=%fused_computation.1 | loop fusion | flops 3072 | bytes 4356 | tf_op jit(solution)/shard_map/add | solution.py:498
  1.5 0.0 copy-start.2
  1.5 0.0 copy-start.3
  1.5 0.0 copy-start.4
  1.5 1.3 %prep.1 = (f32[72,256]{1,0:T(8,128)S(1)}, f32[72,128]{1,0:T(8,128)S(1)}, f32[8,128]{1,0:T(8,128)S(1)}) custom-call(s32[8,128]{1,0:T(8,128)S(1)} %pad_add_fusion.pk_ref, f32[16,32,512]{2,1,0:T(8,128)} %sf_ref.3, f32[32,16,64]{2,1,0:T(8,128)} %sc_ref.1), custom_call_target="tpu_custom_call" | custom-call | tf_op jit(solution)/shard_map/prep/pallas_call | solution.py:503
  2.8 3.1 %collective-permute-start = (f32[72,256]{1,0:T(8,128)S(1)}, f32[72,256]{1,0:T(8,128)S(1)}, u32[]{:S(2)}, u32[]{:S(2)}) collective-permute-start(f32[72,256]{1,0:T(8,128)S(1)} %get-tuple-element.38), channel_id=1, source_target_pairs={{0,16},{1,18},{2,17},{3,19},{4,21},{5,20},{6,23},{7,22},{8,24},{9,... | collective-permute-start | bytes 221192 | tf_op jit(solution)/shard_map/ppermute | solution.py:528
  5.9 3.5 %collective-permute-start.1 = (f32[72,128]{1,0:T(8,128)S(1)}, f32[72,128]{1,0:T(8,128)S(1)}, u32[]{:S(2)}, u32[]{:S(2)}) collective-permute-start(f32[72,128]{1,0:T(8,128)S(1)} %get-tuple-element.39), channel_id=1, source_target_pairs={{0,9},{1,8},{2,11},{3,10},{4,12},{5,14},{6,13},{7,15},{8,1},{9,0},... | collective-permute-start | bytes 110600 | tf_op jit(solution)/shard_map/ppermute | solution.py:529
  9.4 0.0 copy-start.1
  9.4 0.5 %collective-permute-start.2 = (f32[8,128]{1,0:T(8,128)S(1)}, f32[8,128]{1,0:T(8,128)S(1)}, u32[]{:S(2)}, u32[]{:S(2)}) collective-permute-start(f32[8,128]{1,0:T(8,128)S(1)} %get-tuple-element.37.order_ref), channel_id=1, source_target_pairs={{0,24},{4,28},{8,16},{12,20},{16,8},{20,12},{24,0},{28,4},{1,25},{... | collective-permute-start | bytes 12296 | tf_op jit(solution)/shard_map/ppermute | solution.py:532
  9.9 0.0 copy-done
  9.9 0.0 copy-done.2
  9.9 0.0 copy-done.3
  9.9 0.0 copy-done.4
  9.9 0.9 %tables.1 = (f32[14,16,128]{2,1,0:T(8,128)S(1)}, bf16[136,96]{1,0:T(8,128)(2,1)S(1)}, f32[16,128]{1,0:T(8,128)S(1)}, f32[12,136,128]{2,1,0:T(8,128)S(1)}, f32[10...) custom-call(f32[12,64]{1,0:T(8,128)S(1)} %copy-done.3, f32[12,512]{1,0:T(8,128)S(1)} %copy-done.2, ...), custom_call_target="tpu_custom_call" | custom-call | tf_op jit(solution)/shard_map/tables/pallas_call | solution.py:517
  10.8 0.6 %collective-permute-done.1.b_ref = f32[72,128]{1,0:T(8,128)S(1)} collective-permute-done((f32[72,128]{1,0:T(8,128)S(1)}, f32[72,128]{1,0:T(8,128)S(1)}, u32[]{:S(2)}, u32[]{:S(2)}) %collective-permute-start.1) | collective-permute-done | bytes 36896 | tf_op jit(solution)/shard_map/ppermute | solution.py:529
  11.3 0.0 collective-permute-done.a_ref.side_ref
  11.3 2.6 %collective-permute-done.2 = f32[8,128]{1,0:T(8,128)S(1)} collective-permute-done((f32[8,128]{1,0:T(8,128)S(1)}, f32[8,128]{1,0:T(8,128)S(1)}, u32[]{:S(2)}, u32[]{:S(2)}) %collective-permute-start.2) | collective-permute-done | bytes 4128 | tf_op jit(solution)/shard_map/ppermute | solution.py:532
  13.9 0.0 collective-permute-start.3
  13.9 0.0 copy-done.1
  13.9 1.2 %coarse_near.1 = (f32[4,16,64]{2,1,0:T(8,128)S(1)}, f32[8,72,128]{2,1,0:T(8,128)S(1)}) custom-call(f32[10,16,128]{2,1,0:T(8,128)S(1)} %get-tuple-element.40.x_ref, bf16[72,96]{1,0:T(8,128)(2,1)S(1)} %get-tuple-element.41.y_ref, f32[16,128]{1,0:T(8,128)S(1)} %get-tuple-element.42.z_ref, f32[32,16,64]{2,1,0:T(8,128)S(1)} %copy-done.1, ...), custom_call_target="tpu_custom_call" | custom-call | tf_op jit(solution)/shard_map/coarse_near/pallas_call | solution.py:541
  15.1 0.0 collective-permute-done.3.two_ref.twin_ref
  15.1 3.3 %fine_smooth.1 = f32[4,16,64]{2,1,0:T(8,128)S(1)} custom-call(f32[14,16,128]{2,1,0:T(8,128)S(1)} %get-tuple-element.33.x_ref, bf16[136,96]{1,0:T(8,128)(2,1)S(1)} %get-tuple-element.34.y_ref, f32[16,128]{1,0:T(8,128)S(1)} %get-tuple-element.35.z_ref, f32[12,136,128]{2,1,0:T(8,128)S(1)} %get-tuple-element.36.f_ref, ...), custom_call_target="tpu_custom_call" | custom-call | tf_op jit(solution)/shard_map/fine_smooth/pallas_call | solution.py:553
  18.4 1.4 %collective-permute-start.4 = (f32[4,16,64]{2,1,0:T(8,128)S(1)}, f32[4,16,64]{2,1,0:T(8,128)S(1)}, u32[]{:S(2)}, u32[]{:S(2)}) collective-permute-start(f32[4,16,64]{2,1,0:T(8,128)S(1)} %fine_smooth.1), channel_id=1, source_target_pairs={{0,3},{1,14},{2,18},{3,31},{4,7},{5,10},{6,22},{7,27},{8,2},{9,15}... | collective-permute-start | bytes 49160 | tf_op jit(solution)/shard_map/ppermute | solution.py:563
  19.7 1.9 %coarse_far.1 = f32[4,16,64]{2,1,0:T(8,128)S(1)} custom-call(f32[10,16,128]{2,1,0:T(8,128)S(1)} %get-tuple-element.40.x_ref, bf16[72,96]{1,0:T(8,128)(2,1)S(1)} %get-tuple-element.41.y_ref, f32[16,128]{1,0:T(8,128)S(1)} %get-tuple-element.42.z_ref, f32[8,72,128]{2,1,0:T(8,128)S(1)} %get-tuple-element.44.f_ref, ...), custom_call_target="tpu_custom_call" | custom-call | tf_op jit(solution)/shard_map/coarse_far/pallas_call | solution.py:565
  21.6 1.6 %collective-permute-done.4 = f32[4,16,64]{2,1,0:T(8,128)S(1)} collective-permute-done((f32[4,16,64]{2,1,0:T(8,128)S(1)}, f32[4,16,64]{2,1,0:T(8,128)S(1)}, u32[]{:S(2)}, u32[]{:S(2)}) %collective-permute-start.4) | collective-permute-done | bytes 16416 | tf_op jit(solution)/shard_map/ppermute | solution.py:563
  23.2 0.6 %add.23 = f32[4,16,64]{2,1,0:T(8,128)} add(f32[4,16,64]{2,1,0:T(8,128)S(1)} %collective-permute-done.4, f32[4,16,64]{2,1,0:T(8,128)S(1)} %coarse_far.1) | non-fusion elementwise | flops 4096 | bytes 49152 | tf_op jit(solution)/shard_map/add | solution.py:575
  (3 shorter events, 0.0 us)
Async XLA Ops:
  0.0 9.9 %copy-start = (f32[16,32,512]{2,1,0:T(8,128)S(1)}, f32[16,32,512]{2,1,0:T(8,128)}, u32[]{:S(2)}) copy-start(f32[16,32,512]{2,1,0:T(8,128)} %sf_ref.3) | copy-start | bytes 3145732
  1.5 8.4 %copy-start.2 = (f32[12,512]{1,0:T(8,128)S(1)}, f32[12,512]{1,0:T(8,128)}, u32[]{:S(2)}) copy-start(f32[12,512]{1,0:T(8,128)} %my_ref.1) | copy-start | bytes 73732
  1.5 8.4 %copy-start.3 = (f32[12,64]{1,0:T(8,128)S(1)}, f32[12,64]{1,0:T(8,128)}, u32[]{:S(2)}) copy-start(f32[12,64]{1,0:T(8,128)} %mx_ref.1) | copy-start | bytes 9220
  1.5 8.4 %copy-start.4 = (f32[12,32]{1,0:T(8,128)S(1)}, f32[12,32]{1,0:T(8,128)}, u32[]{:S(2)}) copy-start(f32[12,32]{1,0:T(8,128)} %mz_ref.1) | copy-start | bytes 4612
  2.8 8.5 %collective-permute-start = (f32[72,256]{1,0:T(8,128)S(1)}, f32[72,256]{1,0:T(8,128)S(1)}, u32[]{:S(2)}, u32[]{:S(2)}) collective-permute-start(f32[72,256]{1,0:T(8,128)S(1)} %get-tuple-element.38), channel_id=1, source_target_pairs={{0,16},{1,18},{2,17},{3,19},{4,21},{5,20},{6,23},{7,22},{8,24},{9,... | collective-permute-start | bytes 221192 | tf_op jit(solution)/shard_map/ppermute | solution.py:528
  5.9 5.5 %collective-permute-start.1 = (f32[72,128]{1,0:T(8,128)S(1)}, f32[72,128]{1,0:T(8,128)S(1)}, u32[]{:S(2)}, u32[]{:S(2)}) collective-permute-start(f32[72,128]{1,0:T(8,128)S(1)} %get-tuple-element.39), channel_id=1, source_target_pairs={{0,9},{1,8},{2,11},{3,10},{4,12},{5,14},{6,13},{7,15},{8,1},{9,0},... | collective-permute-start | bytes 110600 | tf_op jit(solution)/shard_map/ppermute | solution.py:529
  9.4 4.5 %copy-start.1 = (f32[32,16,64]{2,1,0:T(8,128)S(1)}, f32[32,16,64]{2,1,0:T(8,128)}, u32[]{:S(2)}) copy-start(f32[32,16,64]{2,1,0:T(8,128)} %sc_ref.1) | copy-start | bytes 393220
  9.4 4.5 %collective-permute-start.2 = (f32[8,128]{1,0:T(8,128)S(1)}, f32[8,128]{1,0:T(8,128)S(1)}, u32[]{:S(2)}, u32[]{:S(2)}) collective-permute-start(f32[8,128]{1,0:T(8,128)S(1)} %get-tuple-element.37.order_ref), channel_id=1, source_target_pairs={{0,24},{4,28},{8,16},{12,20},{16,8},{20,12},{24,0},{28,4},{1,25},{... | collective-permute-start | bytes 12296 | tf_op jit(solution)/shard_map/ppermute | solution.py:532
  13.9 1.2 %collective-permute-start.3 = (f32[32,128]{1,0:T(8,128)S(1)}, f32[32,128]{1,0:T(8,128)S(1)}, u32[]{:S(2)}, u32[]{:S(2)}) collective-permute-start(f32[32,128]{1,0:T(8,128)S(1)} %pad_maximum_fusion.par_ref.one_ref), channel_id=1, source_target_pairs={{0,4},{4,0},{8,12},{12,8},{16,20},{20,16},{24,28},{28,24},{1,5},{5... | collective-permute-start | bytes 49160 | tf_op jit(solution)/shard_map/ppermute | solution.py:536
  18.4 4.8 %collective-permute-start.4 = (f32[4,16,64]{2,1,0:T(8,128)S(1)}, f32[4,16,64]{2,1,0:T(8,128)S(1)}, u32[]{:S(2)}, u32[]{:S(2)}) collective-permute-start(f32[4,16,64]{2,1,0:T(8,128)S(1)} %fine_smooth.1), channel_id=1, source_target_pairs={{0,3},{1,14},{2,18},{3,31},{4,7},{5,10},{6,22},{7,27},{8,2},{9,15}... | collective-permute-start | bytes 49160 | tf_op jit(solution)/shard_map/ppermute | solution.py:563
